TPU v7x, 128 devices: a whole 4x4x4 slice. The times are simulated.
128 devices in a mesh: grp: 16 (over z, y), mem: 8 (over x, core).
Axes of the slice: x: 4, y: 4, z: 4, core: 2. Of those that a mesh axis runs over, the one named last changes fastest.
Arguments:
- blocks: bfloat16 [1536, 27, 128, 128], P(('grp', 'mem'))
- prolong: bfloat16 [1536, 128, 128], P(('grp', 'mem'))
- cols: int32 [1536, 27], P(('grp', 'mem')), may hold values from 0 to 11, as said below
- codes: int32 [1536], P(('grp', 'mem')), may hold values from 1 to 15, as said below
Outputs:
- coarse_rows: bfloat16 [1536, 27, 128, 128], P(('grp', 'mem'))
- diag_inverse: float32 [1536, 128, 128], P('grp', 'mem')
Inputs may be any that keep to these rules, and one draw needn't show every extreme that they name: codes is the same for the fine rows in slot s of partition m of every group, and the codes of one device's 12 rows are distinct, so the matching is symmetric and a device pairs with each other group at most once. Entry 13 of every row of cols is the row's own slot.
All inputs are finite; a program needn't handle non-finite values.
Results may differ from a plain program's by a relative error of at most 0.0036.
Values may be sent and summed in bfloat16 or wider, within the bound.
No kernel may reach another device: no remote copies, remote signals or barrier semaphores. Data moves between devices by JAX's collectives and lax.ppermute only.
A program may use at most 128 MiB of HBM per device.

v0:
```python
import functools

import jax
import jax.numpy as jnp
from jax import lax
from jax.experimental import pallas as pl
from jax.experimental.pallas import tpu as pltpu
from jax.sharding import PartitionSpec as P


F32, BF16 = jnp.float32, jnp.bfloat16
DIAG = 13
HALF = 13
LINKS = (1, 3, 4, 12)
ROUNDS = (
    (5, 15, 7, 10),
    (9, 14, 6, 11),
    (10, 7, 5, 15),
    (2, 11, 8, 14),
    (6, 10, 9, 13),
    (14, 2, 11, 8),
    (13, 6, 10, 9),
)
CALLS = (ROUNDS[0], ROUNDS[1], (2, 8, 13))
LAST = {code: r for r, row in enumerate(ROUNDS) for code in row}


def pick(i, values):
    out = jnp.int32(values[0])
    for j, v in enumerate(values[1:], 1):
        out = jnp.where(i == j, jnp.int32(v), out)
    return out


def slot_of(codes_ref, code, rows):
    slot = jnp.int32(0)
    for s in range(rows):
        slot = jnp.where(codes_ref[s] == code, jnp.int32(s), slot)
    return slot


def has_code(codes_ref, code, rows):
    found = codes_ref[0] == code
    for s in range(1, rows):
        found = found | (codes_ref[s] == code)
    return found


def transposed(x):
    return x.astype(F32).T.astype(BF16)


def each_term(slot, ks, cols_ref, block_of, prolong_ref, use):
    left = transposed(prolong_ref[slot])
    for a in range(0, len(ks), 2):
        some = ks[a : a + 2]
        right = [
            jnp.dot(
                block_of(k), prolong_ref[cols_ref[slot, k]], preferred_element_type=F32
            ).astype(BF16)
            for k in some
        ]
        right = right[0] if len(right) == 1 else jnp.concatenate(right, axis=1)
        term = jnp.dot(left, right, preferred_element_type=F32)
        for b, k in enumerate(some):
            use(k, term[:, b * 128 : (b + 1) * 128])


def term_kernel(group, ks, pieces, rows, keep, codes_ref, cols_ref, blocks_ref, prolong_ref, *refs):
    n = len(group)
    outs, buf, sem = refs[: n * len(pieces)], refs[-2], refs[-1]
    owns = refs[n * len(pieces) : -2]
    i = pl.program_id(0)
    code = pick(i, group)
    slot = slot_of(codes_ref, code, rows)

    @pl.when(has_code(codes_ref, code, rows))
    def _():
        def use(k, term):
            at = ks.index(k)
            buf[i, at] = term.astype(BF16)
            if keep:
                owns[at // HALF][0, at % HALF] = term

        each_term(slot, ks, cols_ref, lambda k: blocks_ref[0, k - ks[0]], prolong_ref, use)

    def copies(j):
        for p, (at, count) in enumerate(pieces):
            yield pltpu.make_async_copy(
                buf.at[j, pl.ds(at, count)], outs[j * len(pieces) + p], sem.at[j, p]
            )

    for j in range(n):
        @pl.when(i == j)
        def _():
            for copy in copies(j):
                copy.start()

    @pl.when(i == n - 1)
    def _():
        for j in range(n):
            for copy in copies(j):
                copy.wait()


def terms(group, ks, pieces, codes, cols, blocks, prolong, keep=False):
    rows, _, b, _ = blocks.shape
    n, m, span = len(group), len(ks), ks[-1] + 1 - ks[0]
    spec = pltpu.PrefetchScalarGridSpec(
        num_scalar_prefetch=2,
        grid=(n,),
        in_specs=[
            pl.BlockSpec(
                (pl.Element(1), pl.Element(span), pl.Element(b), pl.Element(b)),
                lambda i, codes, cols: (slot_of(codes, pick(i, group), rows), ks[0], 0, 0),
            ),
            pl.BlockSpec((rows, b, b), lambda i, codes, cols: (0, 0, 0)),
        ],
        out_specs=[pl.BlockSpec(memory_space=pl.ANY)] * (n * len(pieces))
        + [pl.BlockSpec((1, HALF, b, b), lambda i, *_: (i, 0, 0, 0))] * (2 * keep),
        scratch_shapes=[
            pltpu.VMEM((n, m, b, b), BF16),
            pltpu.SemaphoreType.DMA((n, len(pieces))),
        ],
    )
    out = pl.pallas_call(
        functools.partial(term_kernel, group, ks, pieces, rows, keep),
        grid_spec=spec,
        out_shape=[jax.ShapeDtypeStruct((count, b, b), BF16) for _, count in pieces] * n
        + [jax.ShapeDtypeStruct((n, HALF, b, b), F32)] * (2 * keep),
        cost_estimate=pl.CostEstimate(
            flops=n * m * 4 * b**3, bytes_accessed=n * m * b * b * 4, transcendentals=0
        ),
    )(codes, cols, blocks, prolong)
    sent = [out[j * len(pieces) : (j + 1) * len(pieces)] for j in range(n)]
    return (sent, out[n * len(pieces) :]) if keep else sent


def diag_kernel(rows, codes_ref, place_ref, blocks_ref, prolong_ref, send_ref, own_ref):
    for s in range(rows):
        right = jnp.dot(blocks_ref[s, 0], prolong_ref[s], preferred_element_type=F32).astype(BF16)
        term = jnp.dot(transposed(prolong_ref[s]), right, preferred_element_type=F32)
        own_ref[s] = term
        send_ref[place_ref[0] ^ codes_ref[s]] = term.astype(BF16)


def diag_terms(groups, codes, place, blocks, prolong):
    rows, _, b, _ = blocks.shape
    spec = pltpu.PrefetchScalarGridSpec(
        num_scalar_prefetch=2,
        grid=(1,),
        in_specs=[
            pl.BlockSpec((rows, 1, b, b), lambda i, *_: (0, DIAG, 0, 0)),
            pl.BlockSpec((rows, b, b), lambda i, *_: (0, 0, 0)),
        ],
        out_specs=[
            pl.BlockSpec((groups, b, b), lambda i, *_: (0, 0, 0)),
            pl.BlockSpec((rows, b, b), lambda i, *_: (0, 0, 0)),
        ],
    )
    return pl.pallas_call(
        functools.partial(diag_kernel, rows),
        grid_spec=spec,
        out_shape=[
            jax.ShapeDtypeStruct((groups, b, b), BF16),
            jax.ShapeDtypeStruct((rows, b, b), F32),
        ],
        cost_estimate=pl.CostEstimate(
            flops=rows * 4 * b**3, bytes_accessed=rows * b * b * 10, transcendentals=0
        ),
        name="diag_terms",
    )(codes, place, blocks, prolong)


def inverse_kernel(rows, parts, codes_ref, place_ref, own_ref, arrived_ref, coarse_ref, inv_ref):
    b = own_ref.shape[1]
    share = b // parts
    row = lax.broadcasted_iota(jnp.int32, (b, b), 0)
    col = lax.broadcasted_iota(jnp.int32, (b, b), 1)
    on_diag = row == col
    two_eye = jnp.where(on_diag, 2.0, 0.0).astype(F32)
    dot = functools.partial(
        jnp.dot, precision=lax.Precision.HIGHEST, preferred_element_type=F32
    )
    for s in range(rows):
        d = own_ref[s] + arrived_ref[place_ref[0] ^ codes_ref[s]].astype(F32)
        coarse_ref[s, 0] = d.astype(BF16)
        only = jnp.where(on_diag, d, 0.0)
        by_col = 1.0 / jnp.sum(only, axis=0, keepdims=True)
        by_row = 1.0 / jnp.sum(only, axis=1, keepdims=True)
        x = by_row * (two_eye - d * by_col)
        x = dot(x, two_eye - dot(d, x))
        for j in range(parts):
            inv_ref[j, s] = x[j * share : (j + 1) * share]


def inverses(parts, codes, place, own, arrived, width):
    rows, b, _ = own.shape
    spec = pltpu.PrefetchScalarGridSpec(
        num_scalar_prefetch=2,
        grid=(1,),
        in_specs=[
            pl.BlockSpec(own.shape, lambda i, *_: (0, 0, 0)),
            pl.BlockSpec(arrived.shape, lambda i, *_: (0, 0, 0)),
        ],
        out_specs=[
            pl.BlockSpec((rows, 1, b, b), lambda i, *_: (0, DIAG, 0, 0)),
            pl.BlockSpec((parts, rows, b // parts, b), lambda i, *_: (0, 0, 0, 0)),
        ],
    )
    return pl.pallas_call(
        functools.partial(inverse_kernel, rows, parts),
        grid_spec=spec,
        out_shape=[
            jax.ShapeDtypeStruct((rows, width, b, b), BF16),
            jax.ShapeDtypeStruct((parts, rows, b // parts, b), F32),
        ],
        cost_estimate=pl.CostEstimate(
            flops=rows * 24 * b**3, bytes_accessed=rows * b * b * 12, transcendentals=0
        ),
        name="inverses",
    )(codes, place, own, arrived)


def add_kernel(group, ks, rows, codes_ref, cols_ref, prolong_ref, blocks_ref, *refs):
    n = len(group)
    arrived = refs[:n]
    coarse, buf_blocks, buf_out, sem_blocks, sem_out = refs[n + 1 :]
    lo, count = ks[0], ks[-1] + 1 - ks[0]
    slots = [slot_of(codes_ref, code, rows) for code in group]
    found = [has_code(codes_ref, code, rows) for code in group]
    runs = [(a, c) for a, c in ((0, DIAG), (DIAG + 1, HALF)) if a in ks]

    def take(j):
        return pltpu.make_async_copy(
            blocks_ref.at[slots[j], pl.ds(lo, count)], buf_blocks.at[j], sem_blocks.at[j]
        )

    def put(j):
        return [
            pltpu.make_async_copy(
                buf_out.at[j, pl.ds(a - lo, c)], coarse.at[slots[j], pl.ds(a, c)], sem_out.at[j, p]
            )
            for p, (a, c) in enumerate(runs)
        ]

    for j in range(n):
        @pl.when(found[j])
        def _():
            take(j).start()

    for j in range(n):
        @pl.when(found[j])
        def _():
            take(j).wait()

            def use(k, term):
                came = arrived[j][ks.index(k)].astype(F32)
                buf_out[j, k - lo] = (term + came).astype(BF16)

            each_term(
                slots[j],
                ks,
                cols_ref,
                lambda k: buf_blocks[j, k - lo],
                prolong_ref,
                use,
            )
            for copy in put(j):
                copy.start()

    for j in range(n):
        @pl.when(found[j])
        def _():
            for copy in put(j):
                copy.wait()


def add_arrived(group, ks, arrived, codes, cols, blocks, prolong, coarse):
    rows, _, b, _ = blocks.shape
    n, span = len(group), ks[-1] + 1 - ks[0]
    spec = pltpu.PrefetchScalarGridSpec(
        num_scalar_prefetch=2,
        grid=(1,),
        in_specs=[
            pl.BlockSpec((rows, b, b), lambda i, *_: (0, 0, 0)),
            pl.BlockSpec(memory_space=pl.ANY),
        ]
        + [pl.BlockSpec(memory_space=pltpu.VMEM)] * n
        + [pl.BlockSpec(memory_space=pl.ANY)],
        out_specs=pl.BlockSpec(memory_space=pl.ANY),
        scratch_shapes=[
            pltpu.VMEM((n, span, b, b), BF16),
            pltpu.VMEM((n, span, b, b), BF16),
            pltpu.SemaphoreType.DMA((n,)),
            pltpu.SemaphoreType.DMA((n, 2)),
        ],
    )
    return pl.pallas_call(
        functools.partial(add_kernel, group, ks, rows),
        grid_spec=spec,
        out_shape=jax.ShapeDtypeStruct(blocks.shape, BF16),
        input_output_aliases={4 + n: 0},
        cost_estimate=pl.CostEstimate(
            flops=n * len(ks) * 4 * b**3, bytes_accessed=n * span * b * b * 6, transcendentals=0
        ),
    )(codes, cols, prolong, blocks, *arrived, coarse)


def sum_kernel(group, at, rows, codes_ref, own_ref, *refs):
    n = len(group)
    arrived, (coarse, buf, sem) = refs[:n], refs[n + 1 :]
    count = buf.shape[1]
    slots = [slot_of(codes_ref, code, rows) for code in group]
    found = [has_code(codes_ref, code, rows) for code in group]

    def put(j):
        return pltpu.make_async_copy(
            buf.at[j], coarse.at[slots[j], pl.ds(at, count)], sem.at[j]
        )

    for j in range(n):
        @pl.when(found[j])
        def _():
            for k in range(count):
                buf[j, k] = (own_ref[j, k] + arrived[j][k].astype(F32)).astype(BF16)
            put(j).start()

    for j in range(n):
        @pl.when(found[j])
        def _():
            put(j).wait()


def sum_arrived(group, at, own, arrived, codes, coarse):
    rows = codes.shape[0]
    n, count, b, _ = own.shape
    spec = pltpu.PrefetchScalarGridSpec(
        num_scalar_prefetch=1,
        grid=(1,),
        in_specs=[pl.BlockSpec(memory_space=pltpu.VMEM)] * (n + 1)
        + [pl.BlockSpec(memory_space=pl.ANY)],
        out_specs=pl.BlockSpec(memory_space=pl.ANY),
        scratch_shapes=[pltpu.VMEM((n, count, b, b), BF16), pltpu.SemaphoreType.DMA((n,))],
    )
    return pl.pallas_call(
        functools.partial(sum_kernel, group, at, rows),
        grid_spec=spec,
        out_shape=jax.ShapeDtypeStruct(coarse.shape, BF16),
        input_output_aliases={2 + n: 0},
        cost_estimate=pl.CostEstimate(
            flops=n * count * b * b, bytes_accessed=n * count * b * b * 8, transcendentals=0
        ),
    )(codes, own, *arrived, coarse)


def copy_kernel(x_ref, o_ref):
    o_ref[...] = x_ref[...]


def after(value, *others):
    return lax.optimization_barrier((value, *others))[0]


def send(x, link, groups):
    return lax.ppermute(x, "grp", [(g, g ^ link) for g in range(groups)])


def local(blocks, prolong, cols, codes):
    groups, parts = lax.axis_size("grp"), lax.axis_size("mem")
    rows, width, b, _ = blocks.shape
    low, high = tuple(range(DIAG)), tuple(range(DIAG + 1, width))
    off = low + high
    total = len(off)

    held, done = {}, []

    def exchange(r, *ready):
        row = ROUNDS[r]
        moving = [held[code] for code in row]
        if r >= 2:
            moving, ready = lax.optimization_barrier((moving, (done[r - 2], *ready)))
            ready = ready[1:]
        got = [send(x, link, groups) for x, link in zip(moving, LINKS)]
        done.append(got)
        held.update(zip(row, got))
        return ready

    def finish(r, codes, coarse):
        group = tuple(code for code in ROUNDS[r] if LAST[code] == r)
        arrived = [held[code] for code in group]
        return add_arrived(group, off, arrived, codes, cols, blocks, prolong, coarse)

    place = lax.axis_index("grp").astype(jnp.int32).reshape(1)
    gate = codes
    for r in range(2):
        got = terms(CALLS[r], off, ((0, total),), gate, cols, blocks, prolong)
        held.update((code, x[0]) for code, x in zip(CALLS[r], got))
        exchange(r)
        gate = after(codes, got[0][0])
    table, own = diag_terms(groups, gate, place, blocks, prolong)
    table = lax.all_to_all(table, "grp", split_axis=0, concat_axis=0, tiled=True)
    gate = after(codes, own)
    got = terms(CALLS[2], off, ((0, total),), gate, cols, blocks, prolong)
    held.update((code, x[0]) for code, x in zip(CALLS[2], got))
    gate = after(codes, got[0][0])
    halves = ((0, HALF), (HALF, HALF))
    direct, kept = terms(LINKS, off, halves, gate, cols, blocks, prolong, True)

    for r in range(2, 7):
        exchange(r)
    coarse, inv = inverses(parts, codes, place, own, table, width)
    shared = lax.all_to_all(inv, "mem", split_axis=0, concat_axis=0, tiled=True)
    coarse = finish(2, codes, coarse)
    shared = pl.pallas_call(
        copy_kernel,
        in_specs=[pl.BlockSpec(memory_space=pltpu.VMEM)],
        out_shape=jax.ShapeDtypeStruct(shared.shape, F32),
        name="keep",
    )(shared)
    highs, _, coarse = lax.optimization_barrier(([x[1] for x in direct], done[5], coarse))
    lows = [send(x[0], link, groups) for x, link in zip(direct, LINKS)]
    highs = [send(x, link, groups) for x, link in zip(highs, LINKS)]
    coarse = finish(5, codes, coarse)
    coarse = finish(6, after(codes, shared), coarse)
    coarse = sum_arrived(LINKS, 0, kept[0], lows, codes, coarse)
    coarse = sum_arrived(LINKS, DIAG + 1, kept[1], highs, codes, coarse)
    return coarse, shared.reshape(parts * rows, b // parts, b)


def solution(mesh):
    in_specs = (
        P(("grp", "mem"), None, None, None),
        P(("grp", "mem"), None, None),
        P(("grp", "mem"), None),
        P(("grp", "mem")),
    )
    out_specs = (P(("grp", "mem"), None, None, None), P("grp", "mem", None))
    return jax.shard_map(local, mesh=mesh, in_specs=in_specs, out_specs=out_specs, check_vma=False)
```

profile of v0, /device:TPU:1, one launch (start us, length us, event | category | flops | bytes accessed | tf_op | source)
XLA Modules:
  0.0 223.1 jit_solution(9921917120252915769)
XLA Ops:
  0.6 6.9 %shard_map.59 = (bf16[26,128,128]{2,1,0:T(8,128)(2,1)}, bf16[26,128,128]{2,1,0:T(8,128)(2,1)}, bf16[26,128,128]{2,1,0:T(8,128)(2,1)}, bf16[26,128,128]{2,1,0:T(8,128)(2,1)}) custom-call(s32[12]{0:T(128)} %codes_ref.16, s32[12,27]{1,0:T(8,128)} %cols_ref.13, bf16[12,27,128,128]{3,2,1,0:T(8,128)(2,1)} %blocks_ref.15, bf16[12,128,128]{2,1,0:T(8,128)(2,1)} %prolong_ref.15), custom_call_target="tpu_custom_call" | custom-call | flops 872415232 | bytes 6815744 | tf_op jit(solution)/shard_map/pallas_call | solution.py:126
  7.5 4.7 %collective-permute-start.12 = (bf16[26,128,128]{2,1,0:T(8,128)(2,1)}, bf16[26,128,128]{2,1,0:T(8,128)(2,1)}, u32[]{:S(2)}, u32[]{:S(2)}) collective-permute-start(bf16[26,128,128]{2,1,0:T(8,128)(2,1)} %get-tuple-element.82), channel_id=1, source_target_pairs={{0,96},{8,104},{16,112},{24,120},{32,64},{40,72},{48,80},{56,88},{... | collective-permute-start | bytes 2555912 | tf_op jit(solution)/shard_map/ppermute | solution.py:366
  12.2 2.7 %collective-permute-start.15 = (bf16[26,128,128]{2,1,0:T(8,128)(2,1)}, bf16[26,128,128]{2,1,0:T(8,128)(2,1)S(1)}, u32[]{:S(2)}, u32[]{:S(2)}) collective-permute-start(bf16[26,128,128]{2,1,0:T(8,128)(2,1)} %get-tuple-element.84), channel_id=1, source_target_pairs={{0,24},{8,16},{16,8},{24,0},{32,56},{40,48},{48,40},{56,32},{64,88... | collective-permute-start | bytes 2555912 | tf_op jit(solution)/shard_map/ppermute | solution.py:366
  14.9 6.9 %shard_map.60 = (bf16[26,128,128]{2,1,0:T(8,128)(2,1)}, bf16[26,128,128]{2,1,0:T(8,128)(2,1)}, bf16[26,128,128]{2,1,0:T(8,128)(2,1)}, bf16[26,128,128]{2,1,0:T(8,128)(2,1)}) custom-call(s32[12]{0:T(128)} %codes_ref.16, s32[12,27]{1,0:T(8,128)} %cols_ref.13, bf16[12,27,128,128]{3,2,1,0:T(8,128)(2,1)} %blocks_ref.15, bf16[12,128,128]{2,1,0:T(8,128)(2,1)} %prolong_ref.15), custom_call_target="tpu_custom_call" | custom-call | flops 872415232 | bytes 6815744 | tf_op jit(solution)/shard_map/pallas_call | solution.py:126
  22.1 9.6 %collective-permute-done.12 = bf16[26,128,128]{2,1,0:T(8,128)(2,1)} collective-permute-done((bf16[26,128,128]{2,1,0:T(8,128)(2,1)}, bf16[26,128,128]{2,1,0:T(8,128)(2,1)}, u32[]{:S(2)}, u32[]{:S(2)}) %collective-permute-start.12) | collective-permute-done | bytes 852000 | tf_op jit(solution)/shard_map/ppermute | solution.py:366
  31.7 2.7 %collective-permute-start.1 = (bf16[26,128,128]{2,1,0:T(8,128)(2,1)}, bf16[26,128,128]{2,1,0:T(8,128)(2,1)}, u32[]{:S(2)}, u32[]{:S(2)}) collective-permute-start(bf16[26,128,128]{2,1,0:T(8,128)(2,1)} %get-tuple-element.72), channel_id=1, source_target_pairs={{0,24},{8,16},{16,8},{24,0},{32,56},{40,48},{48,40},{56,32},{64,88... | collective-permute-start | bytes 2555912 | tf_op jit(solution)/shard_map/ppermute | solution.py:366
  35.3 2.1 collective-permute-start.16
  37.4 12.5 %collective-permute-done = bf16[26,128,128]{2,1,0:T(8,128)(2,1)} collective-permute-done((bf16[26,128,128]{2,1,0:T(8,128)(2,1)}, bf16[26,128,128]{2,1,0:T(8,128)(2,1)}, u32[]{:S(2)}, u32[]{:S(2)}) %collective-permute-start) | collective-permute-done | bytes 852000 | tf_op jit(solution)/shard_map/ppermute | solution.py:366
  49.9 2.9 %collective-permute-done.1 = bf16[26,128,128]{2,1,0:T(8,128)(2,1)} collective-permute-done((bf16[26,128,128]{2,1,0:T(8,128)(2,1)}, bf16[26,128,128]{2,1,0:T(8,128)(2,1)}, u32[]{:S(2)}, u32[]{:S(2)}) %collective-permute-start.1) | collective-permute-done | bytes 852000 | tf_op jit(solution)/shard_map/ppermute | solution.py:366
  54.7 3.3 %diag_terms.1 = (bf16[16,128,128]{2,1,0:T(8,128)(2,1)}, f32[12,128,128]{2,1,0:T(8,128)}) custom-call(s32[12]{0:T(128)} %codes_ref.16, s32[1]{0:T(128)} %bitcast.place_ref, bf16[12,27,128,128]{3,2,1,0:T(8,128)(2,1)} %blocks_ref.15, bf16[12,128,128]{2,1,0:T(8,128)(2,1)} %prolong_ref.15), custom_call_target="tpu_custom_call" | custom-call | flops 100663296 | bytes 1966080 | tf_op jit(solution)/shard_map/diag_terms/pallas_call | solution.py:161
  58.0 6.3 %shard_map.61 = (bf16[26,128,128]{2,1,0:T(8,128)(2,1)}, bf16[26,128,128]{2,1,0:T(8,128)(2,1)}, bf16[26,128,128]{2,1,0:T(8,128)(2,1)}) custom-call(s32[12]{0:T(128)} %codes_ref.16, s32[12,27]{1,0:T(8,128)} %cols_ref.13, bf16[12,27,128,128]{3,2,1,0:T(8,128)(2,1)} %blocks_ref.15, bf16[12,128,128]{2,1,0:T(8,128)(2,1)} %prolong_ref.15), custom_call_target="tpu_custom_call" | custom-call | flops 654311424 | bytes 5111808 | tf_op jit(solution)/shard_map/pallas_call | solution.py:126
  65.4 5.6 %collective-permute-done.16.refs_0_ = bf16[26,128,128]{2,1,0:T(8,128)(2,1)S(1)} collective-permute-done((bf16[26,128,128]{2,1,0:T(8,128)(2,1)}, bf16[26,128,128]{2,1,0:T(8,128)(2,1)S(1)}, u32[]{:S(2)}, u32[]{:S(2)}) %collective-permute-start.16) | collective-permute-done | bytes 852000 | tf_op jit(solution)/shard_map/ppermute | solution.py:366
  74.5 7.2 %collective-permute-done.27 = bf16[26,128,128]{2,1,0:T(8,128)(2,1)} collective-permute-done((bf16[26,128,128]{2,1,0:T(8,128)(2,1)}, bf16[26,128,128]{2,1,0:T(8,128)(2,1)}, u32[]{:S(2)}, u32[]{:S(2)}) %collective-permute-start.27) | collective-permute-done | bytes 852000 | tf_op jit(solution)/shard_map/ppermute | solution.py:366
  83.7 6.3 %collective-permute-done.4 = bf16[26,128,128]{2,1,0:T(8,128)(2,1)} collective-permute-done((bf16[26,128,128]{2,1,0:T(8,128)(2,1)}, bf16[26,128,128]{2,1,0:T(8,128)(2,1)}, u32[]{:S(2)}, u32[]{:S(2)}) %collective-permute-start.4) | collective-permute-done | bytes 852000 | tf_op jit(solution)/shard_map/ppermute | solution.py:366
  90.0 10.0 %collective-permute-done.5 = bf16[26,128,128]{2,1,0:T(8,128)(2,1)} collective-permute-done((bf16[26,128,128]{2,1,0:T(8,128)(2,1)}, bf16[26,128,128]{2,1,0:T(8,128)(2,1)}, u32[]{:S(2)}, u32[]{:S(2)}) %collective-permute-start.5) | collective-permute-done | bytes 852000 | tf_op jit(solution)/shard_map/ppermute | solution.py:366
  100.0 2.5 %collective-permute-start.30 = (bf16[26,128,128]{2,1,0:T(8,128)(2,1)}, bf16[26,128,128]{2,1,0:T(8,128)(2,1)}, u32[]{:S(2)}, u32[]{:S(2)}) collective-permute-start(bf16[26,128,128]{2,1,0:T(8,128)(2,1)} %collective-permute-done.27), channel_id=1, source_target_pairs={{0,24},{8,16},{16,8},{24,0},{32,56},{40,48},{48,40},{56,32},{64,88... | collective-permute-start | bytes 2555912 | tf_op jit(solution)/shard_map/ppermute | solution.py:366
  102.5 9.1 %shard_map.62 = (bf16[13,128,128]{2,1,0:T(8,128)(2,1)}, bf16[13,128,128]{2,1,0:T(8,128)(2,1)}, bf16[13,128,128]{2,1,0:T(8,128)(2,1)}, bf16[13,128,128]{2,1,0:T(8...) custom-call(s32[12]{0:T(128)} %codes_ref.16, ...), custom_call_target="tpu_custom_call" | custom-call | flops 872415232 | bytes 6815744 | tf_op jit(solution)/shard_map/pallas_call | solution.py:126
  111.7 15.5 %collective-permute-done.23.refs_0_ = bf16[13,128,128]{2,1,0:T(8,128)(2,1)S(1)} collective-permute-done((bf16[13,128,128]{2,1,0:T(8,128)(2,1)}, bf16[13,128,128]{2,1,0:T(8,128)(2,1)S(1)}, u32[]{:S(2)}, u32[]{:S(2)}) %collective-permute-start.23) | collective-permute-done | bytes 426016 | tf_op jit(solution)/shard_map/ppermute | solution.py:366
  127.3 2.8 %collective-permute-start.9 = (bf16[26,128,128]{2,1,0:T(8,128)(2,1)}, bf16[26,128,128]{2,1,0:T(8,128)(2,1)S(1)}, u32[]{:S(2)}, u32[]{:S(2)}) collective-permute-start(bf16[26,128,128]{2,1,0:T(8,128)(2,1)} %collective-permute-done.5), channel_id=1, source_target_pairs={{0,24},{8,16},{16,8},{24,0},{32,56},{40,48},{48,40},{56,32},{64,88... | collective-permute-start | bytes 2555912 | tf_op jit(solution)/shard_map/ppermute | solution.py:366
  130.1 3.3 %collective-permute-start.11 = (bf16[26,128,128]{2,1,0:T(8,128)(2,1)}, bf16[26,128,128]{2,1,0:T(8,128)(2,1)}, u32[]{:S(2)}, u32[]{:S(2)}) collective-permute-start(bf16[26,128,128]{2,1,0:T(8,128)(2,1)} %collective-permute-done.7), channel_id=1, source_target_pairs={{0,96},{8,104},{16,112},{24,120},{32,64},{40,72},{48,80},{56,88},{... | collective-permute-start | bytes 2555912 | tf_op jit(solution)/shard_map/ppermute | solution.py:366
  133.8 3.6 %all-to-all-start = ((bf16[16,128,128]{2,1,0:T(8,128)(2,1)}), bf16[16,128,128]{2,1,0:T(8,128)(2,1)S(1)}, u32[]{:S(2)}, u32[]{:S(2)}) async-start(bf16[16,128,128]{2,1,0:T(8,128)(2,1)} %get-tuple-element.88), calls=%async_computation | async-start | bytes 1048576 | tf_op jit(solution)/shard_map/all_to_all | solution.py:402
  137.4 17.5 %collective-permute-done.24.refs_1_ = bf16[13,128,128]{2,1,0:T(8,128)(2,1)S(1)} collective-permute-done((bf16[13,128,128]{2,1,0:T(8,128)(2,1)}, bf16[13,128,128]{2,1,0:T(8,128)(2,1)S(1)}, u32[]{:S(2)}, u32[]{:S(2)}) %collective-permute-start.24) | collective-permute-done | bytes 426016 | tf_op jit(solution)/shard_map/ppermute | solution.py:366
  155.8 2.6 %collective-permute-start.33 = (bf16[26,128,128]{2,1,0:T(8,128)(2,1)}, bf16[26,128,128]{2,1,0:T(8,128)(2,1)}, u32[]{:S(2)}, u32[]{:S(2)}) collective-permute-start(bf16[26,128,128]{2,1,0:T(8,128)(2,1)} %collective-permute-done.29), channel_id=1, source_target_pairs={{0,24},{8,16},{16,8},{24,0},{32,56},{40,48},{48,40},{56,32},{64,88... | collective-permute-start | bytes 2555912 | tf_op jit(solution)/shard_map/ppermute | solution.py:366
  159.9 5.1 %collective-permute-start.35 = (bf16[26,128,128]{2,1,0:T(8,128)(2,1)}, bf16[26,128,128]{2,1,0:T(8,128)(2,1)}, u32[]{:S(2)}, u32[]{:S(2)}) collective-permute-start(bf16[26,128,128]{2,1,0:T(8,128)(2,1)} %collective-permute-done.31), channel_id=1, source_target_pairs={{0,96},{8,104},{16,112},{24,120},{32,64},{40,72},{48,80},{56,88},{... | collective-permute-start | bytes 2555912 | tf_op jit(solution)/shard_map/ppermute | solution.py:366
  165.9 4.7 %inverses.1 = (bf16[12,27,128,128]{3,2,1,0:T(8,128)(2,1)}, f32[8,12,16,128]{3,2,1,0:T(8,128)}) custom-call(s32[12]{0:T(128)} %codes_ref.16, s32[1]{0:T(128)} %bitcast.place_ref, f32[12,128,128]{2,1,0:T(8,128)} %get-tuple-element.61.own_ref, bf16[16,128,128]{2,1,0:T(8,128)(2,1)} %copy-done.7), custom_call_target="tpu_custom_call" | custom-call | flops 603979776 | bytes 2359296 | tf_op jit(solution)/shard_map/inverses/pallas_call | solution.py:211
  170.6 11.7 %all-to-all-start.1 = ((f32[8,12,16,128]{3,2,1,0:T(8,128)}), f32[8,12,16,128]{3,2,1,0:T(8,128)S(1)}, u32[]{:S(2)}, u32[]{:S(2)}) async-start(f32[8,12,16,128]{3,2,1,0:T(8,128)} %get-tuple-element.99), calls=%async_computation.1 | async-start | bytes 1572864 | tf_op jit(solution)/shard_map/all_to_all | solution.py:413
  182.3 6.9 %shard_map.63.refs_4_ = bf16[12,27,128,128]{3,2,1,0:T(8,128)(2,1)} custom-call(s32[12]{0:T(128)} %codes_ref.16, s32[12,27]{1,0:T(8,128)} %cols_ref.13, bf16[12,128,128]{2,1,0:T(8,128)(2,1)} %prolong_ref.15, bf16[12,27,128,128]{3,2,1,0:T(8,128)(2,1)} %blocks_ref.15, bf16[26,128,128]{2,1,0:T(8,128)(2,1)} %copy-done.4, ...), custom_call_target="tpu_custom_call", output_to_operand_aliasing={{}: (7, {})} | custom-call | flops 654311424 | bytes 7962624 | tf_op jit(solution)/shard_map/pallas_call | solution.py:299
  195.9 2.1 keep.1
  198.0 7.2 %shard_map.64.refs_4_ = bf16[12,27,128,128]{3,2,1,0:T(8,128)(2,1)} custom-call(s32[12]{0:T(128)} %codes_ref.16, s32[12,27]{1,0:T(8,128)} %cols_ref.13, bf16[12,128,128]{2,1,0:T(8,128)(2,1)} %prolong_ref.15, bf16[12,27,128,128]{3,2,1,0:T(8,128)(2,1)} %blocks_ref.15, bf16[26,128,128]{2,1,0:T(8,128)(2,1)} %copy-done.1, ...), custom_call_target="tpu_custom_call", output_to_operand_aliasing={{}: (8, {})} | custom-call | flops 872415232 | bytes 10616832 | tf_op jit(solution)/shard_map/pallas_call | solution.py:299
  205.2 7.2 %shard_map.65.refs_4_ = bf16[12,27,128,128]{3,2,1,0:T(8,128)(2,1)} custom-call(s32[12]{0:T(128)} %codes_ref.16, s32[12,27]{1,0:T(8,128)} %cols_ref.13, bf16[12,128,128]{2,1,0:T(8,128)(2,1)} %prolong_ref.15, bf16[12,27,128,128]{3,2,1,0:T(8,128)(2,1)} %blocks_ref.15, ...), custom_call_target="tpu_custom_call", output_to_operand_aliasing={{}: (8, {})} | custom-call | flops 872415232 | bytes 10616832 | tf_op jit(solution)/shard_map/pallas_call | solution.py:299
  213.2 4.2 %shard_map.66.refs_4_ = bf16[12,27,128,128]{3,2,1,0:T(8,128)(2,1)} custom-call(s32[12]{0:T(128)} %codes_ref.16, f32[4,13,128,128]{3,2,1,0:T(8,128)} %get-tuple-element.94.own_ref, bf16[13,128,128]{2,1,0:T(8,128)(2,1)} %copy-done.8, bf16[13,128,128]{2,1,0:T(8,128)(2,1)} %copy-done.9, ...), custom_call_target="tpu_custom_call", output_to_operand_aliasing={{}: (6, {})} | custom-call | flops 851968 | bytes 6815744 | tf_op jit(solution)/shard_map/pallas_call | solution.py:346
  218.7 4.2 %shard_map.67 = bf16[12,27,128,128]{3,2,1,0:T(8,128)(2,1)} custom-call(s32[12]{0:T(128)} %codes_ref.16, f32[4,13,128,128]{3,2,1,0:T(8,128)} %get-tuple-element.65.own_ref, bf16[13,128,128]{2,1,0:T(8,128)(2,1)} %copy-done.10, bf16[13,128,128]{2,1,0:T(8,128)(2,1)} %copy-done.11, bf16[13,128,128]{2,1,0:T(8,128)(2,1)} %copy-done.13, ...), custom_call_target="tpu_custom_call", output_to_operand_aliasing={{}: (6, {})} | custom-call | flops 851968 | bytes 6815744 | tf_op jit(solution)/shard_map/pallas_call | solution.py:346
  (88 shorter events, 21.8 us)
Async XLA Ops:
  7.5 24.2 %collective-permute-start.12 = (bf16[26,128,128]{2,1,0:T(8,128)(2,1)}, bf16[26,128,128]{2,1,0:T(8,128)(2,1)}, u32[]{:S(2)}, u32[]{:S(2)}) collective-permute-start(bf16[26,128,128]{2,1,0:T(8,128)(2,1)} %get-tuple-element.82), channel_id=1, source_target_pairs={{0,96},{8,104},{16,112},{24,120},{32,64},{40,72},{48,80},{56,88},{... | collective-permute-start | bytes 2555912 | tf_op jit(solution)/shard_map/ppermute | solution.py:366
  12.2 22.3 %collective-permute-start.13 = (bf16[26,128,128]{2,1,0:T(8,128)(2,1)}, bf16[26,128,128]{2,1,0:T(8,128)(2,1)}, u32[]{:S(2)}, u32[]{:S(2)}) collective-permute-start(bf16[26,128,128]{2,1,0:T(8,128)(2,1)} %get-tuple-element.83), channel_id=1, source_target_pairs={{0,32},{8,40},{16,48},{24,56},{32,0},{40,8},{48,16},{56,24},{64,96... | collective-permute-start | bytes 2555912 | tf_op jit(solution)/shard_map/ppermute | solution.py:366
  12.2 22.3 %collective-permute-start.15 = (bf16[26,128,128]{2,1,0:T(8,128)(2,1)}, bf16[26,128,128]{2,1,0:T(8,128)(2,1)S(1)}, u32[]{:S(2)}, u32[]{:S(2)}) collective-permute-start(bf16[26,128,128]{2,1,0:T(8,128)(2,1)} %get-tuple-element.84), channel_id=1, source_target_pairs={{0,24},{8,16},{16,8},{24,0},{32,56},{40,48},{48,40},{56,32},{64,88... | collective-permute-start | bytes 2555912 | tf_op jit(solution)/shard_map/ppermute | solution.py:366
  21.8 28.1 %collective-permute-start = (bf16[26,128,128]{2,1,0:T(8,128)(2,1)}, bf16[26,128,128]{2,1,0:T(8,128)(2,1)}, u32[]{:S(2)}, u32[]{:S(2)}) collective-permute-start(bf16[26,128,128]{2,1,0:T(8,128)(2,1)} %get-tuple-element.70), channel_id=1, source_target_pairs={{0,96},{8,104},{16,112},{24,120},{32,64},{40,72},{48,80},{56,88},{... | collective-permute-start | bytes 2555912 | tf_op jit(solution)/shard_map/ppermute | solution.py:366
  34.4 29.9 %collective-permute-start.3 = (bf16[26,128,128]{2,1,0:T(8,128)(2,1)}, bf16[26,128,128]{2,1,0:T(8,128)(2,1)}, u32[]{:S(2)}, u32[]{:S(2)}) collective-permute-start(bf16[26,128,128]{2,1,0:T(8,128)(2,1)} %get-tuple-element.73), channel_id=1, source_target_pairs={{0,32},{8,40},{16,48},{24,56},{32,0},{40,8},{48,16},{56,24},{64,96... | collective-permute-start | bytes 2555912 | tf_op jit(solution)/shard_map/ppermute | solution.py:366
  34.4 30.0 %collective-permute-start.2 = (bf16[26,128,128]{2,1,0:T(8,128)(2,1)}, bf16[26,128,128]{2,1,0:T(8,128)(2,1)S(1)}, u32[]{:S(2)}, u32[]{:S(2)}) collective-permute-start(bf16[26,128,128]{2,1,0:T(8,128)(2,1)} %get-tuple-element.59), channel_id=1, source_target_pairs={{0,8},{8,0},{16,24},{24,16},{32,40},{40,32},{48,56},{56,48},{64,72... | collective-permute-start | bytes 2555912 | tf_op jit(solution)/shard_map/ppermute | solution.py:366
  35.3 35.7 %collective-permute-start.16 = (bf16[26,128,128]{2,1,0:T(8,128)(2,1)}, bf16[26,128,128]{2,1,0:T(8,128)(2,1)S(1)}, u32[]{:S(2)}, u32[]{:S(2)}) collective-permute-start(bf16[26,128,128]{2,1,0:T(8,128)(2,1)} %collective-permute-done.13), channel_id=1, source_target_pairs={{0,24},{8,16},{16,8},{24,0},{32,56},{40,48},{48,40},{56,32},{64,88... | collective-permute-start | bytes 2555912 | tf_op jit(solution)/shard_map/ppermute | solution.py:366
  49.9 22.3 %collective-permute-start.17 = (bf16[26,128,128]{2,1,0:T(8,128)(2,1)}, bf16[26,128,128]{2,1,0:T(8,128)(2,1)S(1)}, u32[]{:S(2)}, u32[]{:S(2)}) collective-permute-start(bf16[26,128,128]{2,1,0:T(8,128)(2,1)} %collective-permute-done.14), channel_id=1, source_target_pairs={{0,32},{8,40},{16,48},{24,56},{32,0},{40,8},{48,16},{56,24},{64,96... | collective-permute-start | bytes 2555912 | tf_op jit(solution)/shard_map/ppermute | solution.py:366
  64.5 25.5 %collective-permute-start.4 = (bf16[26,128,128]{2,1,0:T(8,128)(2,1)}, bf16[26,128,128]{2,1,0:T(8,128)(2,1)}, u32[]{:S(2)}, u32[]{:S(2)}) collective-permute-start(bf16[26,128,128]{2,1,0:T(8,128)(2,1)} %collective-permute-done.1), channel_id=1, source_target_pairs={{0,96},{8,104},{16,112},{24,120},{32,64},{40,72},{48,80},{56,88},{... | collective-permute-start | bytes 2555912 | tf_op jit(solution)/shard_map/ppermute | solution.py:366
  71.0 29.0 %collective-permute-start.5 = (bf16[26,128,128]{2,1,0:T(8,128)(2,1)}, bf16[26,128,128]{2,1,0:T(8,128)(2,1)}, u32[]{:S(2)}, u32[]{:S(2)}) collective-permute-start(bf16[26,128,128]{2,1,0:T(8,128)(2,1)} %get-tuple-element.75), channel_id=1, source_target_pairs={{0,8},{8,0},{16,24},{24,16},{32,40},{40,32},{48,56},{56,48},{64,72... | collective-permute-start | bytes 2555912 | tf_op jit(solution)/shard_map/ppermute | solution.py:366
  72.2 30.2 %collective-permute-start.6 = (bf16[26,128,128]{2,1,0:T(8,128)(2,1)}, bf16[26,128,128]{2,1,0:T(8,128)(2,1)}, u32[]{:S(2)}, u32[]{:S(2)}) collective-permute-start(bf16[26,128,128]{2,1,0:T(8,128)(2,1)} %collective-permute-done), channel_id=1, source_target_pairs={{0,24},{8,16},{16,8},{24,0},{32,56},{40,48},{48,40},{56,32},{64,88... | collective-permute-start | bytes 2555912 | tf_op jit(solution)/shard_map/ppermute | solution.py:366
  73.8 37.7 %collective-permute-start.7 = (bf16[26,128,128]{2,1,0:T(8,128)(2,1)}, bf16[26,128,128]{2,1,0:T(8,128)(2,1)}, u32[]{:S(2)}, u32[]{:S(2)}) collective-permute-start(bf16[26,128,128]{2,1,0:T(8,128)(2,1)} %get-tuple-element.77), channel_id=1, source_target_pairs={{0,32},{8,40},{16,48},{24,56},{32,0},{40,8},{48,16},{56,24},{64,96... | collective-permute-start | bytes 2555912 | tf_op jit(solution)/shard_map/ppermute | solution.py:366
  81.7 45.6 %collective-permute-start.28 = (bf16[26,128,128]{2,1,0:T(8,128)(2,1)}, bf16[26,128,128]{2,1,0:T(8,128)(2,1)}, u32[]{:S(2)}, u32[]{:S(2)}) collective-permute-start(bf16[26,128,128]{2,1,0:T(8,128)(2,1)} %get-tuple-element.103), channel_id=1, source_target_pairs={{0,96},{8,104},{16,112},{24,120},{32,64},{40,72},{48,80},{56,88},{... | collective-permute-start | bytes 2555912 | tf_op jit(solution)/shard_map/ppermute | solution.py:366
  90.0 40.1 %collective-permute-start.29 = (bf16[26,128,128]{2,1,0:T(8,128)(2,1)}, bf16[26,128,128]{2,1,0:T(8,128)(2,1)}, u32[]{:S(2)}, u32[]{:S(2)}) collective-permute-start(bf16[26,128,128]{2,1,0:T(8,128)(2,1)} %collective-permute-done.3), channel_id=1, source_target_pairs={{0,8},{8,0},{16,24},{24,16},{32,40},{40,32},{48,56},{56,48},{64,72... | collective-permute-start | bytes 2555912 | tf_op jit(solution)/shard_map/ppermute | solution.py:366
  100.0 30.1 %collective-permute-start.30 = (bf16[26,128,128]{2,1,0:T(8,128)(2,1)}, bf16[26,128,128]{2,1,0:T(8,128)(2,1)}, u32[]{:S(2)}, u32[]{:S(2)}) collective-permute-start(bf16[26,128,128]{2,1,0:T(8,128)(2,1)} %collective-permute-done.27), channel_id=1, source_target_pairs={{0,24},{8,16},{16,8},{24,0},{32,56},{40,48},{48,40},{56,32},{64,88... | collective-permute-start | bytes 2555912 | tf_op jit(solution)/shard_map/ppermute | solution.py:366
  102.5 30.9 %collective-permute-start.31 = (bf16[26,128,128]{2,1,0:T(8,128)(2,1)S(1)}, bf16[26,128,128]{2,1,0:T(8,128)(2,1)}, u32[]{:S(2)}, u32[]{:S(2)}) collective-permute-start(bf16[26,128,128]{2,1,0:T(8,128)(2,1)S(1)} %collective-permute-done.2), channel_id=1, source_target_pairs={{0,32},{8,40},{16,48},{24,56},{32,0},{40,8},{48,16},{56,24},{64,96... | collective-permute-start | bytes 2555912 | tf_op jit(solution)/shard_map/ppermute | solution.py:366
  127.3 28.6 %collective-permute-start.8 = (bf16[26,128,128]{2,1,0:T(8,128)(2,1)}, bf16[26,128,128]{2,1,0:T(8,128)(2,1)S(1)}, u32[]{:S(2)}, u32[]{:S(2)}) collective-permute-start(bf16[26,128,128]{2,1,0:T(8,128)(2,1)} %collective-permute-done.4), channel_id=1, source_target_pairs={{0,8},{8,0},{16,24},{24,16},{32,40},{40,32},{48,56},{56,48},{64,72... | collective-permute-start | bytes 2555912 | tf_op jit(solution)/shard_map/ppermute | solution.py:366
  127.3 31.2 %collective-permute-start.9 = (bf16[26,128,128]{2,1,0:T(8,128)(2,1)}, bf16[26,128,128]{2,1,0:T(8,128)(2,1)S(1)}, u32[]{:S(2)}, u32[]{:S(2)}) collective-permute-start(bf16[26,128,128]{2,1,0:T(8,128)(2,1)} %collective-permute-done.5), channel_id=1, source_target_pairs={{0,24},{8,16},{16,8},{24,0},{32,56},{40,48},{48,40},{56,32},{64,88... | collective-permute-start | bytes 2555912 | tf_op jit(solution)/shard_map/ppermute | solution.py:366
  130.0 29.9 %collective-permute-start.10 = (bf16[26,128,128]{2,1,0:T(8,128)(2,1)}, bf16[26,128,128]{2,1,0:T(8,128)(2,1)S(1)}, u32[]{:S(2)}, u32[]{:S(2)}) collective-permute-start(bf16[26,128,128]{2,1,0:T(8,128)(2,1)} %collective-permute-done.6), channel_id=1, source_target_pairs={{0,32},{8,40},{16,48},{24,56},{32,0},{40,8},{48,16},{56,24},{64,96... | collective-permute-start | bytes 2555912 | tf_op jit(solution)/shard_map/ppermute | solution.py:366
  130.1 35.0 %collective-permute-start.11 = (bf16[26,128,128]{2,1,0:T(8,128)(2,1)}, bf16[26,128,128]{2,1,0:T(8,128)(2,1)}, u32[]{:S(2)}, u32[]{:S(2)}) collective-permute-start(bf16[26,128,128]{2,1,0:T(8,128)(2,1)} %collective-permute-done.7), channel_id=1, source_target_pairs={{0,96},{8,104},{16,112},{24,120},{32,64},{40,72},{48,80},{56,88},{... | collective-permute-start | bytes 2555912 | tf_op jit(solution)/shard_map/ppermute | solution.py:366
  133.8 31.2 %all-to-all-start = ((bf16[16,128,128]{2,1,0:T(8,128)(2,1)}), bf16[16,128,128]{2,1,0:T(8,128)(2,1)S(1)}, u32[]{:S(2)}, u32[]{:S(2)}) async-start(bf16[16,128,128]{2,1,0:T(8,128)(2,1)} %get-tuple-element.88), calls=%async_computation | async-start | bytes 1048576 | tf_op jit(solution)/shard_map/all_to_all | solution.py:402
  154.9 35.7 %collective-permute-start.32 = (bf16[26,128,128]{2,1,0:T(8,128)(2,1)}, bf16[26,128,128]{2,1,0:T(8,128)(2,1)}, u32[]{:S(2)}, u32[]{:S(2)}) collective-permute-start(bf16[26,128,128]{2,1,0:T(8,128)(2,1)} %collective-permute-done.28), channel_id=1, source_target_pairs={{0,8},{8,0},{16,24},{24,16},{32,40},{40,32},{48,56},{56,48},{64,72... | collective-permute-start | bytes 2555912 | tf_op jit(solution)/shard_map/ppermute | solution.py:366
  155.8 35.8 %collective-permute-start.33 = (bf16[26,128,128]{2,1,0:T(8,128)(2,1)}, bf16[26,128,128]{2,1,0:T(8,128)(2,1)}, u32[]{:S(2)}, u32[]{:S(2)}) collective-permute-start(bf16[26,128,128]{2,1,0:T(8,128)(2,1)} %collective-permute-done.29), channel_id=1, source_target_pairs={{0,24},{8,16},{16,8},{24,0},{32,56},{40,48},{48,40},{56,32},{64,88... | collective-permute-start | bytes 2555912 | tf_op jit(solution)/shard_map/ppermute | solution.py:366
  158.5 34.7 %collective-permute-start.34 = (bf16[26,128,128]{2,1,0:T(8,128)(2,1)}, bf16[26,128,128]{2,1,0:T(8,128)(2,1)}, u32[]{:S(2)}, u32[]{:S(2)}) collective-permute-start(bf16[26,128,128]{2,1,0:T(8,128)(2,1)} %collective-permute-done.30), channel_id=1, source_target_pairs={{0,32},{8,40},{16,48},{24,56},{32,0},{40,8},{48,16},{56,24},{64,96... | collective-permute-start | bytes 2555912 | tf_op jit(solution)/shard_map/ppermute | solution.py:366
  159.9 34.4 %collective-permute-start.35 = (bf16[26,128,128]{2,1,0:T(8,128)(2,1)}, bf16[26,128,128]{2,1,0:T(8,128)(2,1)}, u32[]{:S(2)}, u32[]{:S(2)}) collective-permute-start(bf16[26,128,128]{2,1,0:T(8,128)(2,1)} %collective-permute-done.31), channel_id=1, source_target_pairs={{0,96},{8,104},{16,112},{24,120},{32,64},{40,72},{48,80},{56,88},{... | collective-permute-start | bytes 2555912 | tf_op jit(solution)/shard_map/ppermute | solution.py:366
  165.0 24.2 %collective-permute-start.25 = (bf16[13,128,128]{2,1,0:T(8,128)(2,1)}, bf16[13,128,128]{2,1,0:T(8,128)(2,1)}, u32[]{:S(2)}, u32[]{:S(2)}) collective-permute-start(bf16[13,128,128]{2,1,0:T(8,128)(2,1)} %get-tuple-element.97), channel_id=1, source_target_pairs={{0,32},{8,40},{16,48},{24,56},{32,0},{40,8},{48,16},{56,24},{64,96... | collective-permute-start | bytes 1277960 | tf_op jit(solution)/shard_map/ppermute | solution.py:366
  170.6 24.4 %all-to-all-start.1 = ((f32[8,12,16,128]{3,2,1,0:T(8,128)}), f32[8,12,16,128]{3,2,1,0:T(8,128)S(1)}, u32[]{:S(2)}, u32[]{:S(2)}) async-start(f32[8,12,16,128]{3,2,1,0:T(8,128)} %get-tuple-element.99), calls=%async_computation.1 | async-start | bytes 1572864 | tf_op jit(solution)/shard_map/all_to_all | solution.py:413
  189.3 23.2 %collective-permute-start.26 = (bf16[13,128,128]{2,1,0:T(8,128)(2,1)}, bf16[13,128,128]{2,1,0:T(8,128)(2,1)S(1)}, u32[]{:S(2)}, u32[]{:S(2)}) collective-permute-start(bf16[13,128,128]{2,1,0:T(8,128)(2,1)} %get-tuple-element.98), channel_id=1, source_target_pairs={{0,96},{8,104},{16,112},{24,120},{32,64},{40,72},{48,80},{56,88},{... | collective-permute-start | bytes 1277960 | tf_op jit(solution)/shard_map/ppermute | solution.py:366
  190.6 26.9 %collective-permute-start.19 = (bf16[13,128,128]{2,1,0:T(8,128)(2,1)}, bf16[13,128,128]{2,1,0:T(8,128)(2,1)S(1)}, u32[]{:S(2)}, u32[]{:S(2)}) collective-permute-start(bf16[13,128,128]{2,1,0:T(8,128)(2,1)} %get-tuple-element.90), channel_id=1, source_target_pairs={{0,8},{8,0},{16,24},{24,16},{32,40},{40,32},{48,56},{56,48},{64,72... | collective-permute-start | bytes 1277960 | tf_op jit(solution)/shard_map/ppermute | solution.py:366
  191.6 25.8 %collective-permute-start.20 = (bf16[13,128,128]{2,1,0:T(8,128)(2,1)}, bf16[13,128,128]{2,1,0:T(8,128)(2,1)S(1)}, u32[]{:S(2)}, u32[]{:S(2)}) collective-permute-start(bf16[13,128,128]{2,1,0:T(8,128)(2,1)} %get-tuple-element.91), channel_id=1, source_target_pairs={{0,24},{8,16},{16,8},{24,0},{32,56},{40,48},{48,40},{56,32},{64,88... | collective-permute-start | bytes 1277960 | tf_op jit(solution)/shard_map/ppermute | solution.py:366
  193.2 24.3 %collective-permute-start.21 = (bf16[13,128,128]{2,1,0:T(8,128)(2,1)}, bf16[13,128,128]{2,1,0:T(8,128)(2,1)S(1)}, u32[]{:S(2)}, u32[]{:S(2)}) collective-permute-start(bf16[13,128,128]{2,1,0:T(8,128)(2,1)} %get-tuple-element.92), channel_id=1, source_target_pairs={{0,32},{8,40},{16,48},{24,56},{32,0},{40,8},{48,16},{56,24},{64,96... | collective-permute-start | bytes 1277960 | tf_op jit(solution)/shard_map/ppermute | solution.py:366
  194.3 23.2 %collective-permute-start.22 = (bf16[13,128,128]{2,1,0:T(8,128)(2,1)}, bf16[13,128,128]{2,1,0:T(8,128)(2,1)S(1)}, u32[]{:S(2)}, u32[]{:S(2)}) collective-permute-start(bf16[13,128,128]{2,1,0:T(8,128)(2,1)} %get-tuple-element.93), channel_id=1, source_target_pairs={{0,96},{8,104},{16,112},{24,120},{32,64},{40,72},{48,80},{56,88},{... | collective-permute-start | bytes 1277960 | tf_op jit(solution)/shard_map/ppermute | solution.py:366
  (22 other events, 369.9 us)
where the time goes:
time: 227 us; the launch traced here: 223 us
  waiting for transfers between devices  88.4 us (39%)
  Pallas kernels  69.2 us (30%)
  starting transfers between devices  59.9 us (26%)
  local copies, waits for them, and re-layouts  4.44 us (2%)
    ppermute x36, waiting for transfers between devices, send(): return lax.ppermute(x, 'grp', [(g, g ^ link) for g in range(groups)])  88.4 us
    ppermute x36, starting transfers between devices, send(): return lax.ppermute(x, 'grp', [(g, g ^ link) for g in range(groups)])  44.6 us
    pallas_call x4, Pallas kernels, terms(): pl.pallas_call(functools.partial(term_kernel, group, ks, pieces, rows, ke...  29.2 us
    pallas_call x3, Pallas kernels, add_arrived(): pl.pallas_call(functools.partial(add_kernel, group, ks, rows), grid_spec=...  21.4 us
    all_to_all x1, starting transfers between devices, local(): shared = lax.all_to_all(inv, 'mem', split_axis=0, concat_axis=0, tiled=True)  11.7 us
    pallas_call x2, Pallas kernels, sum_arrived(): pl.pallas_call(functools.partial(sum_kernel, group, at, rows), grid_spec=...  8.45 us
    pallas_call x1, Pallas kernels, inverses(): pl.pallas_call(functools.partial(inverse_kernel, rows, parts), grid_spec=...  4.71 us
  transfers between devices with their start and end apart: 38, of which 10 were waited for; matrix products, arithmetic and copies ran while one was open for 0% of the time, Pallas kernels for 26%

commit v1 on v0

--- a/solution.py
+++ b/solution.py
@@ -9,6 +9,7 @@
 
 
 F32, BF16 = jnp.float32, jnp.bfloat16
+PARAMS = pltpu.CompilerParams(vmem_limit_bytes=36 * 2**20)
 DIAG = 13
 HALF = 13
 LINKS = (1, 3, 4, 12)
@@ -276,7 +277,7 @@
                 copy.wait()
 
 
-def add_arrived(group, ks, arrived, codes, cols, blocks, prolong, coarse):
+def add_arrived(group, ks, arrived, codes, cols, blocks, prolong, coarse, at_hand):
     rows, _, b, _ = blocks.shape
     n, span = len(group), ks[-1] + 1 - ks[0]
     spec = pltpu.PrefetchScalarGridSpec(
@@ -301,10 +302,18 @@
         grid_spec=spec,
         out_shape=jax.ShapeDtypeStruct(blocks.shape, BF16),
         input_output_aliases={4 + n: 0},
+        compiler_params=PARAMS,
         cost_estimate=pl.CostEstimate(
             flops=n * len(ks) * 4 * b**3, bytes_accessed=n * span * b * b * 6, transcendentals=0
         ),
-    )(codes, cols, prolong, blocks, *arrived, coarse)
+    )(
+        far(codes),
+        far(cols),
+        far(prolong),
+        far(blocks),
+        *(near(x) if at_hand else x for x in arrived),
+        far(coarse),
+    )
 
 
 def sum_kernel(group, at, rows, codes_ref, own_ref, *refs):
@@ -348,14 +357,23 @@
         grid_spec=spec,
         out_shape=jax.ShapeDtypeStruct(coarse.shape, BF16),
         input_output_aliases={2 + n: 0},
+        compiler_params=PARAMS,
         cost_estimate=pl.CostEstimate(
             flops=n * count * b * b, bytes_accessed=n * count * b * b * 8, transcendentals=0
         ),
-    )(codes, own, *arrived, coarse)
+    )(far(codes), near(own), *map(near, arrived), far(coarse))
 
 
 def copy_kernel(x_ref, o_ref):
     o_ref[...] = x_ref[...]
+
+
+def near(x):
+    return pltpu.with_memory_space_constraint(x, pltpu.VMEM)
+
+
+def far(x):
+    return pltpu.with_memory_space_constraint(x, pltpu.HBM)
 
 
 def after(value, *others):
@@ -389,7 +407,7 @@
     def finish(r, codes, coarse):
         group = tuple(code for code in ROUNDS[r] if LAST[code] == r)
         arrived = [held[code] for code in group]
-        return add_arrived(group, off, arrived, codes, cols, blocks, prolong, coarse)
+        return add_arrived(group, off, arrived, codes, cols, blocks, prolong, coarse, r > 2)
 
     place = lax.axis_index("grp").astype(jnp.int32).reshape(1)
     gate = codes
@@ -417,7 +435,7 @@
         in_specs=[pl.BlockSpec(memory_space=pltpu.VMEM)],
         out_shape=jax.ShapeDtypeStruct(shared.shape, F32),
         name="keep",
-    )(shared)
+    )(near(shared))
     highs, _, coarse = lax.optimization_barrier(([x[1] for x in direct], done[5], coarse))
     lows = [send(x[0], link, groups) for x, link in zip(direct, LINKS)]
     highs = [send(x, link, groups) for x, link in zip(highs, LINKS)]

time: 227 us -> 224 us (0.987); the launches traced: 223 us -> 223 us
  Pallas kernels: 69.2 us -> 65.2 us
  local copies, waits for them, and re-layouts: 4.44 us -> 7.96 us
  waiting for transfers between devices: 88.4 us -> 90.8 us
    unnamed x32 -> x40, local copies, waits for them, and re-layouts: 4.44 us -> 7.96 us
    ppermute x36, waiting for transfers between devices: 88.4 us -> 90.7 us  [send(): return lax.ppermute(x, 'grp', [(g, g ^ link) for g in range(groups)])]
  transfers between devices with their start and end apart: 38 -> 38, of which waited for: 10 -> 10; matrix products, arithmetic and copies ran while one was open for 0% -> 0% of each run, Pallas kernels for 26% -> 25%
where the time goes in v1:
time: 224 us; the launch traced here: 223 us
  waiting for transfers between devices  90.8 us (41%)
  Pallas kernels  65.2 us (29%)
  starting transfers between devices  57.7 us (26%)
  local copies, waits for them, and re-layouts  7.96 us (4%)
    ppermute x36, waiting for transfers between devices, send(): return lax.ppermute(x, 'grp', [(g, g ^ link) for g in range(groups)])  90.7 us
    ppermute x36, starting transfers between devices, send(): return lax.ppermute(x, 'grp', [(g, g ^ link) for g in range(groups)])  43.5 us
    pallas_call x4, Pallas kernels, terms(): pl.pallas_call(functools.partial(term_kernel, group, ks, pieces, rows, ke...  29.4 us
    pallas_call x3, Pallas kernels, add_arrived(): pl.pallas_call(functools.partial(add_kernel, group, ks, rows), grid_spec=...  20.4 us
    all_to_all x1, starting transfers between devices, local(): shared = lax.all_to_all(inv, 'mem', split_axis=0, concat_axis=0, tiled=True)  10.2 us
    unnamed x40, local copies, waits for them, and re-layouts  7.96 us
    pallas_call x2, Pallas kernels, sum_arrived(): pl.pallas_call(functools.partial(sum_kernel, group, at, rows), grid_spec=...  6.37 us
    pallas_call x1, Pallas kernels, inverses(): pl.pallas_call(functools.partial(inverse_kernel, rows, parts), grid_spec=...  4.72 us
  transfers between devices with their start and end apart: 38, of which 10 were waited for; matrix products, arithmetic and copies ran while one was open for 0% of the time, Pallas kernels for 25%

profile of v1, /device:TPU:1, one launch (start us, length us, event | category | flops | bytes accessed | tf_op | source)
XLA Modules:
  0.0 222.7 jit_solution(6952613021610664339)
XLA Ops:
  0.6 6.9 %shard_map.59 = (bf16[26,128,128]{2,1,0:T(8,128)(2,1)}, bf16[26,128,128]{2,1,0:T(8,128)(2,1)}, bf16[26,128,128]{2,1,0:T(8,128)(2,1)}, bf16[26,128,128]{2,1,0:T(8,128)(2,1)}) custom-call(s32[12]{0:T(128)} %codes_ref.16, s32[12,27]{1,0:T(8,128)} %cols_ref.13, bf16[12,27,128,128]{3,2,1,0:T(8,128)(2,1)} %blocks_ref.15, bf16[12,128,128]{2,1,0:T(8,128)(2,1)} %prolong_ref.15), custom_call_target="tpu_custom_call" | custom-call | flops 872415232 | bytes 6815744 | tf_op jit(solution)/shard_map/pallas_call | solution.py:127
  7.5 4.7 %collective-permute-start.12 = (bf16[26,128,128]{2,1,0:T(8,128)(2,1)}, bf16[26,128,128]{2,1,0:T(8,128)(2,1)S(1)}, u32[]{:S(2)}, u32[]{:S(2)}) collective-permute-start(bf16[26,128,128]{2,1,0:T(8,128)(2,1)} %get-tuple-element.82), channel_id=1, source_target_pairs={{0,96},{8,104},{16,112},{24,120},{32,64},{40,72},{48,80},{56,88},{... | collective-permute-start | bytes 2555912 | tf_op jit(solution)/shard_map/ppermute | solution.py:384
  12.2 2.7 %collective-permute-start.15 = (bf16[26,128,128]{2,1,0:T(8,128)(2,1)}, bf16[26,128,128]{2,1,0:T(8,128)(2,1)S(1)}, u32[]{:S(2)}, u32[]{:S(2)}) collective-permute-start(bf16[26,128,128]{2,1,0:T(8,128)(2,1)} %get-tuple-element.84), channel_id=1, source_target_pairs={{0,24},{8,16},{16,8},{24,0},{32,56},{40,48},{48,40},{56,32},{64,88... | collective-permute-start | bytes 2555912 | tf_op jit(solution)/shard_map/ppermute | solution.py:384
  14.9 6.9 %shard_map.60 = (bf16[26,128,128]{2,1,0:T(8,128)(2,1)}, bf16[26,128,128]{2,1,0:T(8,128)(2,1)}, bf16[26,128,128]{2,1,0:T(8,128)(2,1)}, bf16[26,128,128]{2,1,0:T(8,128)(2,1)}) custom-call(s32[12]{0:T(128)} %codes_ref.16, s32[12,27]{1,0:T(8,128)} %cols_ref.13, bf16[12,27,128,128]{3,2,1,0:T(8,128)(2,1)} %blocks_ref.15, bf16[12,128,128]{2,1,0:T(8,128)(2,1)} %prolong_ref.15), custom_call_target="tpu_custom_call" | custom-call | flops 872415232 | bytes 6815744 | tf_op jit(solution)/shard_map/pallas_call | solution.py:127
  22.1 9.6 %collective-permute-done.12 = bf16[26,128,128]{2,1,0:T(8,128)(2,1)S(1)} collective-permute-done((bf16[26,128,128]{2,1,0:T(8,128)(2,1)}, bf16[26,128,128]{2,1,0:T(8,128)(2,1)S(1)}, u32[]{:S(2)}, u32[]{:S(2)}) %collective-permute-start.12) | collective-permute-done | bytes 852000 | tf_op jit(solution)/shard_map/ppermute | solution.py:384
  31.7 2.7 %collective-permute-start.1 = (bf16[26,128,128]{2,1,0:T(8,128)(2,1)}, bf16[26,128,128]{2,1,0:T(8,128)(2,1)S(1)}, u32[]{:S(2)}, u32[]{:S(2)}) collective-permute-start(bf16[26,128,128]{2,1,0:T(8,128)(2,1)} %get-tuple-element.72), channel_id=1, source_target_pairs={{0,24},{8,16},{16,8},{24,0},{32,56},{40,48},{48,40},{56,32},{64,88... | collective-permute-start | bytes 2555912 | tf_op jit(solution)/shard_map/ppermute | solution.py:384
  36.7 13.3 %collective-permute-done = bf16[26,128,128]{2,1,0:T(8,128)(2,1)} collective-permute-done((bf16[26,128,128]{2,1,0:T(8,128)(2,1)}, bf16[26,128,128]{2,1,0:T(8,128)(2,1)}, u32[]{:S(2)}, u32[]{:S(2)}) %collective-permute-start) | collective-permute-done | bytes 852000 | tf_op jit(solution)/shard_map/ppermute | solution.py:384
  50.0 2.8 %collective-permute-done.1 = bf16[26,128,128]{2,1,0:T(8,128)(2,1)S(1)} collective-permute-done((bf16[26,128,128]{2,1,0:T(8,128)(2,1)}, bf16[26,128,128]{2,1,0:T(8,128)(2,1)S(1)}, u32[]{:S(2)}, u32[]{:S(2)}) %collective-permute-start.1) | collective-permute-done | bytes 852000 | tf_op jit(solution)/shard_map/ppermute | solution.py:384
  55.6 3.3 %diag_terms.1 = (bf16[16,128,128]{2,1,0:T(8,128)(2,1)}, f32[12,128,128]{2,1,0:T(8,128)}) custom-call(s32[12]{0:T(128)} %codes_ref.16, s32[1]{0:T(128)} %bitcast.place_ref, bf16[12,27,128,128]{3,2,1,0:T(8,128)(2,1)} %blocks_ref.15, bf16[12,128,128]{2,1,0:T(8,128)(2,1)} %prolong_ref.15), custom_call_target="tpu_custom_call" | custom-call | flops 100663296 | bytes 1966080 | tf_op jit(solution)/shard_map/diag_terms/pallas_call | solution.py:162
  58.9 6.4 %shard_map.61 = (bf16[26,128,128]{2,1,0:T(8,128)(2,1)}, bf16[26,128,128]{2,1,0:T(8,128)(2,1)}, bf16[26,128,128]{2,1,0:T(8,128)(2,1)}) custom-call(s32[12]{0:T(128)} %codes_ref.16, s32[12,27]{1,0:T(8,128)} %cols_ref.13, bf16[12,27,128,128]{3,2,1,0:T(8,128)(2,1)} %blocks_ref.15, bf16[12,128,128]{2,1,0:T(8,128)(2,1)} %prolong_ref.15), custom_call_target="tpu_custom_call" | custom-call | flops 654311424 | bytes 5111808 | tf_op jit(solution)/shard_map/pallas_call | solution.py:127
  66.3 4.8 %collective-permute-done.16.refs_0_ = bf16[26,128,128]{2,1,0:T(8,128)(2,1)S(1)} collective-permute-done((bf16[26,128,128]{2,1,0:T(8,128)(2,1)}, bf16[26,128,128]{2,1,0:T(8,128)(2,1)S(1)}, u32[]{:S(2)}, u32[]{:S(2)}) %collective-permute-start.16) | collective-permute-done | bytes 852000 | tf_op jit(solution)/shard_map/ppermute | solution.py:384
  74.7 8.2 %collective-permute-done.27 = bf16[26,128,128]{2,1,0:T(8,128)(2,1)} collective-permute-done((bf16[26,128,128]{2,1,0:T(8,128)(2,1)}, bf16[26,128,128]{2,1,0:T(8,128)(2,1)}, u32[]{:S(2)}, u32[]{:S(2)}) %collective-permute-start.27) | collective-permute-done | bytes 852000 | tf_op jit(solution)/shard_map/ppermute | solution.py:384
  82.9 2.0 collective-permute-start.28
  84.8 6.3 %collective-permute-done.4 = bf16[26,128,128]{2,1,0:T(8,128)(2,1)} collective-permute-done((bf16[26,128,128]{2,1,0:T(8,128)(2,1)}, bf16[26,128,128]{2,1,0:T(8,128)(2,1)}, u32[]{:S(2)}, u32[]{:S(2)}) %collective-permute-start.4) | collective-permute-done | bytes 852000 | tf_op jit(solution)/shard_map/ppermute | solution.py:384
  91.2 9.9 %collective-permute-done.5 = bf16[26,128,128]{2,1,0:T(8,128)(2,1)} collective-permute-done((bf16[26,128,128]{2,1,0:T(8,128)(2,1)}, bf16[26,128,128]{2,1,0:T(8,128)(2,1)}, u32[]{:S(2)}, u32[]{:S(2)}) %collective-permute-start.5) | collective-permute-done | bytes 852000 | tf_op jit(solution)/shard_map/ppermute | solution.py:384
  101.1 2.5 %collective-permute-start.30 = (bf16[26,128,128]{2,1,0:T(8,128)(2,1)}, bf16[26,128,128]{2,1,0:T(8,128)(2,1)}, u32[]{:S(2)}, u32[]{:S(2)}) collective-permute-start(bf16[26,128,128]{2,1,0:T(8,128)(2,1)} %collective-permute-done.27), channel_id=1, source_target_pairs={{0,24},{8,16},{16,8},{24,0},{32,56},{40,48},{48,40},{56,32},{64,88... | collective-permute-start | bytes 2555912 | tf_op jit(solution)/shard_map/ppermute | solution.py:384
  103.6 9.3 %shard_map.62 = (bf16[13,128,128]{2,1,0:T(8,128)(2,1)}, bf16[13,128,128]{2,1,0:T(8,128)(2,1)}, bf16[13,128,128]{2,1,0:T(8,128)(2,1)}, bf16[13,128,128]{2,1,0:T(8...) custom-call(s32[12]{0:T(128)} %codes_ref.16, ...), custom_call_target="tpu_custom_call" | custom-call | flops 872415232 | bytes 6815744 | tf_op jit(solution)/shard_map/pallas_call | solution.py:127
  113.0 15.4 %collective-permute-done.23.refs_0_ = bf16[13,128,128]{2,1,0:T(8,128)(2,1)S(1)} collective-permute-done((bf16[13,128,128]{2,1,0:T(8,128)(2,1)}, bf16[13,128,128]{2,1,0:T(8,128)(2,1)S(1)}, u32[]{:S(2)}, u32[]{:S(2)}) %collective-permute-start.23) | collective-permute-done | bytes 426016 | tf_op jit(solution)/shard_map/ppermute | solution.py:384
  129.2 2.7 %collective-permute-start.9 = (bf16[26,128,128]{2,1,0:T(8,128)(2,1)}, bf16[26,128,128]{2,1,0:T(8,128)(2,1)S(1)}, u32[]{:S(2)}, u32[]{:S(2)}) collective-permute-start(bf16[26,128,128]{2,1,0:T(8,128)(2,1)} %collective-permute-done.5), channel_id=1, source_target_pairs={{0,24},{8,16},{16,8},{24,0},{32,56},{40,48},{48,40},{56,32},{64,88... | collective-permute-start | bytes 2555912 | tf_op jit(solution)/shard_map/ppermute | solution.py:384
  132.0 3.4 %collective-permute-start.11 = (bf16[26,128,128]{2,1,0:T(8,128)(2,1)}, bf16[26,128,128]{2,1,0:T(8,128)(2,1)}, u32[]{:S(2)}, u32[]{:S(2)}) collective-permute-start(bf16[26,128,128]{2,1,0:T(8,128)(2,1)} %collective-permute-done.7), channel_id=1, source_target_pairs={{0,96},{8,104},{16,112},{24,120},{32,64},{40,72},{48,80},{56,88},{... | collective-permute-start | bytes 2555912 | tf_op jit(solution)/shard_map/ppermute | solution.py:384
  135.5 4.0 %all-to-all-start = ((bf16[16,128,128]{2,1,0:T(8,128)(2,1)}), bf16[16,128,128]{2,1,0:T(8,128)(2,1)S(1)}, u32[]{:S(2)}, u32[]{:S(2)}) async-start(bf16[16,128,128]{2,1,0:T(8,128)(2,1)} %get-tuple-element.88), calls=%async_computation | async-start | bytes 1048576 | tf_op jit(solution)/shard_map/all_to_all | solution.py:420
  139.5 19.2 %collective-permute-done.24.refs_1_ = bf16[13,128,128]{2,1,0:T(8,128)(2,1)S(1)} collective-permute-done((bf16[13,128,128]{2,1,0:T(8,128)(2,1)}, bf16[13,128,128]{2,1,0:T(8,128)(2,1)S(1)}, u32[]{:S(2)}, u32[]{:S(2)}) %collective-permute-start.24) | collective-permute-done | bytes 426016 | tf_op jit(solution)/shard_map/ppermute | solution.py:384
  159.2 2.4 %collective-permute-start.33 = (bf16[26,128,128]{2,1,0:T(8,128)(2,1)}, bf16[26,128,128]{2,1,0:T(8,128)(2,1)}, u32[]{:S(2)}, u32[]{:S(2)}) collective-permute-start(bf16[26,128,128]{2,1,0:T(8,128)(2,1)} %collective-permute-done.29), channel_id=1, source_target_pairs={{0,24},{8,16},{16,8},{24,0},{32,56},{40,48},{48,40},{56,32},{64,88... | collective-permute-start | bytes 2555912 | tf_op jit(solution)/shard_map/ppermute | solution.py:384
  162.6 4.8 %collective-permute-start.35 = (bf16[26,128,128]{2,1,0:T(8,128)(2,1)}, bf16[26,128,128]{2,1,0:T(8,128)(2,1)}, u32[]{:S(2)}, u32[]{:S(2)}) collective-permute-start(bf16[26,128,128]{2,1,0:T(8,128)(2,1)} %collective-permute-done.31), channel_id=1, source_target_pairs={{0,96},{8,104},{16,112},{24,120},{32,64},{40,72},{48,80},{56,88},{... | collective-permute-start | bytes 2555912 | tf_op jit(solution)/shard_map/ppermute | solution.py:384
  168.2 4.7 %inverses.1 = (bf16[12,27,128,128]{3,2,1,0:T(8,128)(2,1)}, f32[8,12,16,128]{3,2,1,0:T(8,128)}) custom-call(s32[12]{0:T(128)} %codes_ref.16, s32[1]{0:T(128)} %bitcast.place_ref, f32[12,128,128]{2,1,0:T(8,128)} %get-tuple-element.61.own_ref, bf16[16,128,128]{2,1,0:T(8,128)(2,1)} %copy-done.14), custom_call_target="tpu_custom_call" | custom-call | flops 603979776 | bytes 2359296 | tf_op jit(solution)/shard_map/inverses/pallas_call | solution.py:212
  172.9 10.2 %all-to-all-start.1 = ((f32[8,12,16,128]{3,2,1,0:T(8,128)}), f32[8,12,16,128]{3,2,1,0:T(8,128)S(1)}, u32[]{:S(2)}, u32[]{:S(2)}) async-start(f32[8,12,16,128]{3,2,1,0:T(8,128)} %get-tuple-element.99), calls=%async_computation.1 | async-start | bytes 1572864 | tf_op jit(solution)/shard_map/all_to_all | solution.py:431
  186.6 6.3 %shard_map.63.refs_4_ = bf16[12,27,128,128]{3,2,1,0:T(8,128)(2,1)} custom-call(s32[12]{0:T(128)} %codes_ref.16, s32[12,27]{1,0:T(8,128)} %cols_ref.13, bf16[12,128,128]{2,1,0:T(8,128)(2,1)} %prolong_ref.15, bf16[12,27,128,128]{3,2,1,0:T(8,128)(2,1)} %blocks_ref.15, bf16[26,128,128]{2,1,0:T(8,128)(2,1)S(1)} %copy-done.5, ...), custom_call_target="tpu_custom_call", output_to_operand_aliasing={{}: (7, {})} | custom-call | flops 654311424 | bytes 7962624 | tf_op jit(solution)/shard_map/pallas_call | solution.py:300
  192.9 2.1 collective-permute-start.26
  201.8 6.5 %shard_map.64.refs_4_ = bf16[12,27,128,128]{3,2,1,0:T(8,128)(2,1)} custom-call(s32[12]{0:T(128)} %codes_ref.16, s32[12,27]{1,0:T(8,128)} %cols_ref.13, bf16[12,128,128]{2,1,0:T(8,128)(2,1)} %prolong_ref.15, bf16[12,27,128,128]{3,2,1,0:T(8,128)(2,1)} %blocks_ref.15, ...), custom_call_target="tpu_custom_call", output_to_operand_aliasing={{}: (8, {})} | custom-call | flops 872415232 | bytes 10616832 | tf_op jit(solution)/shard_map/pallas_call | solution.py:300
  208.3 7.7 %shard_map.65.refs_4_ = bf16[12,27,128,128]{3,2,1,0:T(8,128)(2,1)} custom-call(s32[12]{0:T(128)} %codes_ref.16, s32[12,27]{1,0:T(8,128)} %cols_ref.13, bf16[12,128,128]{2,1,0:T(8,128)(2,1)} %prolong_ref.15, bf16[12,27,128,128]{3,2,1,0:T(8,128)(2,1)} %blocks_ref.15, ...), custom_call_target="tpu_custom_call", output_to_operand_aliasing={{}: (8, {})} | custom-call | flops 872415232 | bytes 10616832 | tf_op jit(solution)/shard_map/pallas_call | solution.py:300
  216.1 3.3 %shard_map.66.refs_4_ = bf16[12,27,128,128]{3,2,1,0:T(8,128)(2,1)} custom-call(s32[12]{0:T(128)} %codes_ref.16, f32[4,13,128,128]{3,2,1,0:T(8,128)S(1)} %copy-done.1, bf16[13,128,128]{2,1,0:T(8,128)(2,1)S(1)} %copy-done.11, bf16[13,128,128]{2,1,0:T(8,128)(2,1)S(1)} %copy-done.13, ...), custom_call_target="tpu_custom_call", output_to_operand_aliasing={{}: (6, {})} | custom-call | flops 851968 | bytes 6815744 | tf_op jit(solution)/shard_map/pallas_call | solution.py:355
  219.4 3.1 %shard_map.67 = bf16[12,27,128,128]{3,2,1,0:T(8,128)(2,1)} custom-call(s32[12]{0:T(128)} %codes_ref.16, f32[4,13,128,128]{3,2,1,0:T(8,128)S(1)} %copy-done, bf16[13,128,128]{2,1,0:T(8,128)(2,1)S(1)} %collective-permute-done.19.refs_0_, bf16[13,128,128]{2,1,0:T(8,128)(2,1)} %collective-permute-done.20.refs_1_, ...), custom_call_target="tpu_custom_call", output_to_operand_aliasing={{}: (6, {})} | custom-call | flops 851968 | bytes 6815744 | tf_op jit(solution)/shard_map/pallas_call | solution.py:355
  (96 shorter events, 23.7 us)
Async XLA Ops:
  7.5 24.1 %collective-permute-start.12 = (bf16[26,128,128]{2,1,0:T(8,128)(2,1)}, bf16[26,128,128]{2,1,0:T(8,128)(2,1)S(1)}, u32[]{:S(2)}, u32[]{:S(2)}) collective-permute-start(bf16[26,128,128]{2,1,0:T(8,128)(2,1)} %get-tuple-element.82), channel_id=1, source_target_pairs={{0,96},{8,104},{16,112},{24,120},{32,64},{40,72},{48,80},{56,88},{... | collective-permute-start | bytes 2555912 | tf_op jit(solution)/shard_map/ppermute | solution.py:384
  12.2 22.2 %collective-permute-start.13 = (bf16[26,128,128]{2,1,0:T(8,128)(2,1)}, bf16[26,128,128]{2,1,0:T(8,128)(2,1)S(1)}, u32[]{:S(2)}, u32[]{:S(2)}) collective-permute-start(bf16[26,128,128]{2,1,0:T(8,128)(2,1)} %get-tuple-element.83), channel_id=1, source_target_pairs={{0,32},{8,40},{16,48},{24,56},{32,0},{40,8},{48,16},{56,24},{64,96... | collective-permute-start | bytes 2555912 | tf_op jit(solution)/shard_map/ppermute | solution.py:384
  12.2 22.2 %collective-permute-start.15 = (bf16[26,128,128]{2,1,0:T(8,128)(2,1)}, bf16[26,128,128]{2,1,0:T(8,128)(2,1)S(1)}, u32[]{:S(2)}, u32[]{:S(2)}) collective-permute-start(bf16[26,128,128]{2,1,0:T(8,128)(2,1)} %get-tuple-element.84), channel_id=1, source_target_pairs={{0,24},{8,16},{16,8},{24,0},{32,56},{40,48},{48,40},{56,32},{64,88... | collective-permute-start | bytes 2555912 | tf_op jit(solution)/shard_map/ppermute | solution.py:384
  21.8 28.2 %collective-permute-start = (bf16[26,128,128]{2,1,0:T(8,128)(2,1)}, bf16[26,128,128]{2,1,0:T(8,128)(2,1)}, u32[]{:S(2)}, u32[]{:S(2)}) collective-permute-start(bf16[26,128,128]{2,1,0:T(8,128)(2,1)} %get-tuple-element.70), channel_id=1, source_target_pairs={{0,96},{8,104},{16,112},{24,120},{32,64},{40,72},{48,80},{56,88},{... | collective-permute-start | bytes 2555912 | tf_op jit(solution)/shard_map/ppermute | solution.py:384
  34.4 30.9 %collective-permute-start.3 = (bf16[26,128,128]{2,1,0:T(8,128)(2,1)}, bf16[26,128,128]{2,1,0:T(8,128)(2,1)}, u32[]{:S(2)}, u32[]{:S(2)}) collective-permute-start(bf16[26,128,128]{2,1,0:T(8,128)(2,1)} %get-tuple-element.73), channel_id=1, source_target_pairs={{0,32},{8,40},{16,48},{24,56},{32,0},{40,8},{48,16},{56,24},{64,96... | collective-permute-start | bytes 2555912 | tf_op jit(solution)/shard_map/ppermute | solution.py:384
  34.4 31.0 %collective-permute-start.2 = (bf16[26,128,128]{2,1,0:T(8,128)(2,1)}, bf16[26,128,128]{2,1,0:T(8,128)(2,1)S(1)}, u32[]{:S(2)}, u32[]{:S(2)}) collective-permute-start(bf16[26,128,128]{2,1,0:T(8,128)(2,1)} %get-tuple-element.59), channel_id=1, source_target_pairs={{0,8},{8,0},{16,24},{24,16},{32,40},{40,32},{48,56},{56,48},{64,72... | collective-permute-start | bytes 2555912 | tf_op jit(solution)/shard_map/ppermute | solution.py:384
  35.3 35.8 %collective-permute-start.16 = (bf16[26,128,128]{2,1,0:T(8,128)(2,1)}, bf16[26,128,128]{2,1,0:T(8,128)(2,1)S(1)}, u32[]{:S(2)}, u32[]{:S(2)}) collective-permute-start(bf16[26,128,128]{2,1,0:T(8,128)(2,1)} %copy-done.18), channel_id=1, source_target_pairs={{0,24},{8,16},{16,8},{24,0},{32,56},{40,48},{48,40},{56,32},{64,88... | collective-permute-start | bytes 2555912 | tf_op jit(solution)/shard_map/ppermute | solution.py:384
  50.0 22.3 %collective-permute-start.17 = (bf16[26,128,128]{2,1,0:T(8,128)(2,1)}, bf16[26,128,128]{2,1,0:T(8,128)(2,1)S(1)}, u32[]{:S(2)}, u32[]{:S(2)}) collective-permute-start(bf16[26,128,128]{2,1,0:T(8,128)(2,1)} %collective-permute-done.14), channel_id=1, source_target_pairs={{0,32},{8,40},{16,48},{24,56},{32,0},{40,8},{48,16},{56,24},{64,96... | collective-permute-start | bytes 2555912 | tf_op jit(solution)/shard_map/ppermute | solution.py:384
  65.5 25.7 %collective-permute-start.4 = (bf16[26,128,128]{2,1,0:T(8,128)(2,1)}, bf16[26,128,128]{2,1,0:T(8,128)(2,1)}, u32[]{:S(2)}, u32[]{:S(2)}) collective-permute-start(bf16[26,128,128]{2,1,0:T(8,128)(2,1)} %copy-done.17), channel_id=1, source_target_pairs={{0,96},{8,104},{16,112},{24,120},{32,64},{40,72},{48,80},{56,88},{... | collective-permute-start | bytes 2555912 | tf_op jit(solution)/shard_map/ppermute | solution.py:384
  71.1 30.0 %collective-permute-start.5 = (bf16[26,128,128]{2,1,0:T(8,128)(2,1)}, bf16[26,128,128]{2,1,0:T(8,128)(2,1)}, u32[]{:S(2)}, u32[]{:S(2)}) collective-permute-start(bf16[26,128,128]{2,1,0:T(8,128)(2,1)} %get-tuple-element.75), channel_id=1, source_target_pairs={{0,8},{8,0},{16,24},{24,16},{32,40},{40,32},{48,56},{56,48},{64,72... | collective-permute-start | bytes 2555912 | tf_op jit(solution)/shard_map/ppermute | solution.py:384
  72.3 31.3 %collective-permute-start.6 = (bf16[26,128,128]{2,1,0:T(8,128)(2,1)}, bf16[26,128,128]{2,1,0:T(8,128)(2,1)}, u32[]{:S(2)}, u32[]{:S(2)}) collective-permute-start(bf16[26,128,128]{2,1,0:T(8,128)(2,1)} %collective-permute-done), channel_id=1, source_target_pairs={{0,24},{8,16},{16,8},{24,0},{32,56},{40,48},{48,40},{56,32},{64,88... | collective-permute-start | bytes 2555912 | tf_op jit(solution)/shard_map/ppermute | solution.py:384
  73.9 39.0 %collective-permute-start.7 = (bf16[26,128,128]{2,1,0:T(8,128)(2,1)}, bf16[26,128,128]{2,1,0:T(8,128)(2,1)}, u32[]{:S(2)}, u32[]{:S(2)}) collective-permute-start(bf16[26,128,128]{2,1,0:T(8,128)(2,1)} %get-tuple-element.77), channel_id=1, source_target_pairs={{0,32},{8,40},{16,48},{24,56},{32,0},{40,8},{48,16},{56,24},{64,96... | collective-permute-start | bytes 2555912 | tf_op jit(solution)/shard_map/ppermute | solution.py:384
  82.9 46.4 %collective-permute-start.28 = (bf16[26,128,128]{2,1,0:T(8,128)(2,1)}, bf16[26,128,128]{2,1,0:T(8,128)(2,1)}, u32[]{:S(2)}, u32[]{:S(2)}) collective-permute-start(bf16[26,128,128]{2,1,0:T(8,128)(2,1)} %get-tuple-element.103), channel_id=1, source_target_pairs={{0,96},{8,104},{16,112},{24,120},{32,64},{40,72},{48,80},{56,88},{... | collective-permute-start | bytes 2555912 | tf_op jit(solution)/shard_map/ppermute | solution.py:384
  91.1 40.8 %collective-permute-start.29 = (bf16[26,128,128]{2,1,0:T(8,128)(2,1)}, bf16[26,128,128]{2,1,0:T(8,128)(2,1)}, u32[]{:S(2)}, u32[]{:S(2)}) collective-permute-start(bf16[26,128,128]{2,1,0:T(8,128)(2,1)} %collective-permute-done.3), channel_id=1, source_target_pairs={{0,8},{8,0},{16,24},{24,16},{32,40},{40,32},{48,56},{56,48},{64,72... | collective-permute-start | bytes 2555912 | tf_op jit(solution)/shard_map/ppermute | solution.py:384
  101.1 30.9 %collective-permute-start.30 = (bf16[26,128,128]{2,1,0:T(8,128)(2,1)}, bf16[26,128,128]{2,1,0:T(8,128)(2,1)}, u32[]{:S(2)}, u32[]{:S(2)}) collective-permute-start(bf16[26,128,128]{2,1,0:T(8,128)(2,1)} %collective-permute-done.27), channel_id=1, source_target_pairs={{0,24},{8,16},{16,8},{24,0},{32,56},{40,48},{48,40},{56,32},{64,88... | collective-permute-start | bytes 2555912 | tf_op jit(solution)/shard_map/ppermute | solution.py:384
  103.6 31.8 %collective-permute-start.31 = (bf16[26,128,128]{2,1,0:T(8,128)(2,1)S(1)}, bf16[26,128,128]{2,1,0:T(8,128)(2,1)}, u32[]{:S(2)}, u32[]{:S(2)}) collective-permute-start(bf16[26,128,128]{2,1,0:T(8,128)(2,1)S(1)} %collective-permute-done.2), channel_id=1, source_target_pairs={{0,32},{8,40},{16,48},{24,56},{32,0},{40,8},{48,16},{56,24},{64,96... | collective-permute-start | bytes 2555912 | tf_op jit(solution)/shard_map/ppermute | solution.py:384
  129.2 30.0 %collective-permute-start.8 = (bf16[26,128,128]{2,1,0:T(8,128)(2,1)}, bf16[26,128,128]{2,1,0:T(8,128)(2,1)S(1)}, u32[]{:S(2)}, u32[]{:S(2)}) collective-permute-start(bf16[26,128,128]{2,1,0:T(8,128)(2,1)} %collective-permute-done.4), channel_id=1, source_target_pairs={{0,8},{8,0},{16,24},{24,16},{32,40},{40,32},{48,56},{56,48},{64,72... | collective-permute-start | bytes 2555912 | tf_op jit(solution)/shard_map/ppermute | solution.py:384
  129.2 32.4 %collective-permute-start.9 = (bf16[26,128,128]{2,1,0:T(8,128)(2,1)}, bf16[26,128,128]{2,1,0:T(8,128)(2,1)S(1)}, u32[]{:S(2)}, u32[]{:S(2)}) collective-permute-start(bf16[26,128,128]{2,1,0:T(8,128)(2,1)} %collective-permute-done.5), channel_id=1, source_target_pairs={{0,24},{8,16},{16,8},{24,0},{32,56},{40,48},{48,40},{56,32},{64,88... | collective-permute-start | bytes 2555912 | tf_op jit(solution)/shard_map/ppermute | solution.py:384
  132.0 30.6 %collective-permute-start.10 = (bf16[26,128,128]{2,1,0:T(8,128)(2,1)}, bf16[26,128,128]{2,1,0:T(8,128)(2,1)S(1)}, u32[]{:S(2)}, u32[]{:S(2)}) collective-permute-start(bf16[26,128,128]{2,1,0:T(8,128)(2,1)} %collective-permute-done.6), channel_id=1, source_target_pairs={{0,32},{8,40},{16,48},{24,56},{32,0},{40,8},{48,16},{56,24},{64,96... | collective-permute-start | bytes 2555912 | tf_op jit(solution)/shard_map/ppermute | solution.py:384
  132.0 35.3 %collective-permute-start.11 = (bf16[26,128,128]{2,1,0:T(8,128)(2,1)}, bf16[26,128,128]{2,1,0:T(8,128)(2,1)}, u32[]{:S(2)}, u32[]{:S(2)}) collective-permute-start(bf16[26,128,128]{2,1,0:T(8,128)(2,1)} %collective-permute-done.7), channel_id=1, source_target_pairs={{0,96},{8,104},{16,112},{24,120},{32,64},{40,72},{48,80},{56,88},{... | collective-permute-start | bytes 2555912 | tf_op jit(solution)/shard_map/ppermute | solution.py:384
  135.4 23.3 %collective-permute-start.24 = (bf16[13,128,128]{2,1,0:T(8,128)(2,1)}, bf16[13,128,128]{2,1,0:T(8,128)(2,1)S(1)}, u32[]{:S(2)}, u32[]{:S(2)}) collective-permute-start(bf16[13,128,128]{2,1,0:T(8,128)(2,1)} %get-tuple-element.96), channel_id=1, source_target_pairs={{0,24},{8,16},{16,8},{24,0},{32,56},{40,48},{48,40},{56,32},{64,88... | collective-permute-start | bytes 1277960 | tf_op jit(solution)/shard_map/ppermute | solution.py:384
  135.5 31.9 %all-to-all-start = ((bf16[16,128,128]{2,1,0:T(8,128)(2,1)}), bf16[16,128,128]{2,1,0:T(8,128)(2,1)S(1)}, u32[]{:S(2)}, u32[]{:S(2)}) async-start(bf16[16,128,128]{2,1,0:T(8,128)(2,1)} %get-tuple-element.88), calls=%async_computation | async-start | bytes 1048576 | tf_op jit(solution)/shard_map/all_to_all | solution.py:420
  158.7 36.3 %collective-permute-start.32 = (bf16[26,128,128]{2,1,0:T(8,128)(2,1)}, bf16[26,128,128]{2,1,0:T(8,128)(2,1)}, u32[]{:S(2)}, u32[]{:S(2)}) collective-permute-start(bf16[26,128,128]{2,1,0:T(8,128)(2,1)} %collective-permute-done.28), channel_id=1, source_target_pairs={{0,8},{8,0},{16,24},{24,16},{32,40},{40,32},{48,56},{56,48},{64,72... | collective-permute-start | bytes 2555912 | tf_op jit(solution)/shard_map/ppermute | solution.py:384
  159.2 36.9 %collective-permute-start.33 = (bf16[26,128,128]{2,1,0:T(8,128)(2,1)}, bf16[26,128,128]{2,1,0:T(8,128)(2,1)}, u32[]{:S(2)}, u32[]{:S(2)}) collective-permute-start(bf16[26,128,128]{2,1,0:T(8,128)(2,1)} %collective-permute-done.29), channel_id=1, source_target_pairs={{0,24},{8,16},{16,8},{24,0},{32,56},{40,48},{48,40},{56,32},{64,88... | collective-permute-start | bytes 2555912 | tf_op jit(solution)/shard_map/ppermute | solution.py:384
  161.6 36.3 %collective-permute-start.34 = (bf16[26,128,128]{2,1,0:T(8,128)(2,1)}, bf16[26,128,128]{2,1,0:T(8,128)(2,1)}, u32[]{:S(2)}, u32[]{:S(2)}) collective-permute-start(bf16[26,128,128]{2,1,0:T(8,128)(2,1)} %collective-permute-done.30), channel_id=1, source_target_pairs={{0,32},{8,40},{16,48},{24,56},{32,0},{40,8},{48,16},{56,24},{64,96... | collective-permute-start | bytes 2555912 | tf_op jit(solution)/shard_map/ppermute | solution.py:384
  162.6 36.5 %collective-permute-start.35 = (bf16[26,128,128]{2,1,0:T(8,128)(2,1)}, bf16[26,128,128]{2,1,0:T(8,128)(2,1)}, u32[]{:S(2)}, u32[]{:S(2)}) collective-permute-start(bf16[26,128,128]{2,1,0:T(8,128)(2,1)} %collective-permute-done.31), channel_id=1, source_target_pairs={{0,96},{8,104},{16,112},{24,120},{32,64},{40,72},{48,80},{56,88},{... | collective-permute-start | bytes 2555912 | tf_op jit(solution)/shard_map/ppermute | solution.py:384
  167.4 25.5 %collective-permute-start.25 = (bf16[13,128,128]{2,1,0:T(8,128)(2,1)}, bf16[13,128,128]{2,1,0:T(8,128)(2,1)}, u32[]{:S(2)}, u32[]{:S(2)}) collective-permute-start(bf16[13,128,128]{2,1,0:T(8,128)(2,1)} %get-tuple-element.97), channel_id=1, source_target_pairs={{0,32},{8,40},{16,48},{24,56},{32,0},{40,8},{48,16},{56,24},{64,96... | collective-permute-start | bytes 1277960 | tf_op jit(solution)/shard_map/ppermute | solution.py:384
  172.9 26.8 %all-to-all-start.1 = ((f32[8,12,16,128]{3,2,1,0:T(8,128)}), f32[8,12,16,128]{3,2,1,0:T(8,128)S(1)}, u32[]{:S(2)}, u32[]{:S(2)}) async-start(f32[8,12,16,128]{3,2,1,0:T(8,128)} %get-tuple-element.99), calls=%async_computation.1 | async-start | bytes 1572864 | tf_op jit(solution)/shard_map/all_to_all | solution.py:431
  192.9 23.1 %collective-permute-start.26 = (bf16[13,128,128]{2,1,0:T(8,128)(2,1)}, bf16[13,128,128]{2,1,0:T(8,128)(2,1)}, u32[]{:S(2)}, u32[]{:S(2)}) collective-permute-start(bf16[13,128,128]{2,1,0:T(8,128)(2,1)} %get-tuple-element.98), channel_id=1, source_target_pairs={{0,96},{8,104},{16,112},{24,120},{32,64},{40,72},{48,80},{56,88},{... | collective-permute-start | bytes 1277960 | tf_op jit(solution)/shard_map/ppermute | solution.py:384
  195.0 24.4 %collective-permute-start.19 = (bf16[13,128,128]{2,1,0:T(8,128)(2,1)}, bf16[13,128,128]{2,1,0:T(8,128)(2,1)S(1)}, u32[]{:S(2)}, u32[]{:S(2)}) collective-permute-start(bf16[13,128,128]{2,1,0:T(8,128)(2,1)} %get-tuple-element.90), channel_id=1, source_target_pairs={{0,8},{8,0},{16,24},{24,16},{32,40},{40,32},{48,56},{56,48},{64,72... | collective-permute-start | bytes 1277960 | tf_op jit(solution)/shard_map/ppermute | solution.py:384
  196.1 23.3 %collective-permute-start.20 = (bf16[13,128,128]{2,1,0:T(8,128)(2,1)}, bf16[13,128,128]{2,1,0:T(8,128)(2,1)}, u32[]{:S(2)}, u32[]{:S(2)}) collective-permute-start(bf16[13,128,128]{2,1,0:T(8,128)(2,1)} %get-tuple-element.91), channel_id=1, source_target_pairs={{0,24},{8,16},{16,8},{24,0},{32,56},{40,48},{48,40},{56,32},{64,88... | collective-permute-start | bytes 1277960 | tf_op jit(solution)/shard_map/ppermute | solution.py:384
  197.9 21.5 %collective-permute-start.21 = (bf16[13,128,128]{2,1,0:T(8,128)(2,1)}, bf16[13,128,128]{2,1,0:T(8,128)(2,1)}, u32[]{:S(2)}, u32[]{:S(2)}) collective-permute-start(bf16[13,128,128]{2,1,0:T(8,128)(2,1)} %get-tuple-element.92), channel_id=1, source_target_pairs={{0,32},{8,40},{16,48},{24,56},{32,0},{40,8},{48,16},{56,24},{64,96... | collective-permute-start | bytes 1277960 | tf_op jit(solution)/shard_map/ppermute | solution.py:384
  (26 other events, 348.1 us)

commit v2 on v1

--- a/solution.py
+++ b/solution.py
@@ -81,7 +81,7 @@
             at = ks.index(k)
             buf[i, at] = term.astype(BF16)
             if keep:
-                owns[at // HALF][0, at % HALF] = term
+                owns[0][0, at] = term
 
         each_term(slot, ks, cols_ref, lambda k: blocks_ref[0, k - ks[0]], prolong_ref, use)
 
@@ -118,7 +118,7 @@
             pl.BlockSpec((rows, b, b), lambda i, codes, cols: (0, 0, 0)),
         ],
         out_specs=[pl.BlockSpec(memory_space=pl.ANY)] * (n * len(pieces))
-        + [pl.BlockSpec((1, HALF, b, b), lambda i, *_: (i, 0, 0, 0))] * (2 * keep),
+        + [pl.BlockSpec((1, m, b, b), lambda i, *_: (i, 0, 0, 0))] * keep,
         scratch_shapes=[
             pltpu.VMEM((n, m, b, b), BF16),
             pltpu.SemaphoreType.DMA((n, len(pieces))),
@@ -128,7 +128,7 @@
         functools.partial(term_kernel, group, ks, pieces, rows, keep),
         grid_spec=spec,
         out_shape=[jax.ShapeDtypeStruct((count, b, b), BF16) for _, count in pieces] * n
-        + [jax.ShapeDtypeStruct((n, HALF, b, b), F32)] * (2 * keep),
+        + [jax.ShapeDtypeStruct((n, m, b, b), F32)] * keep,
         cost_estimate=pl.CostEstimate(
             flops=n * m * 4 * b**3, bytes_accessed=n * m * b * b * 4, transcendentals=0
         ),
@@ -316,7 +316,7 @@
     )
 
 
-def sum_kernel(group, at, rows, codes_ref, own_ref, *refs):
+def sum_kernel(group, runs, rows, codes_ref, own_ref, *refs):
     n = len(group)
     arrived, (coarse, buf, sem) = refs[:n], refs[n + 1 :]
     count = buf.shape[1]
@@ -324,24 +324,29 @@
     found = [has_code(codes_ref, code, rows) for code in group]
 
     def put(j):
-        return pltpu.make_async_copy(
-            buf.at[j], coarse.at[slots[j], pl.ds(at, count)], sem.at[j]
-        )
+        return [
+            pltpu.make_async_copy(
+                buf.at[j, pl.ds(p * HALF, HALF)], coarse.at[slots[j], pl.ds(at, HALF)], sem.at[j, p]
+            )
+            for p, at in enumerate(runs)
+        ]
 
     for j in range(n):
         @pl.when(found[j])
         def _():
             for k in range(count):
                 buf[j, k] = (own_ref[j, k] + arrived[j][k].astype(F32)).astype(BF16)
-            put(j).start()
+                if k % HALF == HALF - 1:
+                    put(j)[k // HALF].start()
 
     for j in range(n):
         @pl.when(found[j])
         def _():
-            put(j).wait()
-
-
-def sum_arrived(group, at, own, arrived, codes, coarse):
+            for copy in put(j):
+                copy.wait()
+
+
+def sum_arrived(group, runs, own, arrived, codes, coarse):
     rows = codes.shape[0]
     n, count, b, _ = own.shape
     spec = pltpu.PrefetchScalarGridSpec(
@@ -350,10 +355,13 @@
         in_specs=[pl.BlockSpec(memory_space=pltpu.VMEM)] * (n + 1)
         + [pl.BlockSpec(memory_space=pl.ANY)],
         out_specs=pl.BlockSpec(memory_space=pl.ANY),
-        scratch_shapes=[pltpu.VMEM((n, count, b, b), BF16), pltpu.SemaphoreType.DMA((n,))],
+        scratch_shapes=[
+            pltpu.VMEM((n, count, b, b), BF16),
+            pltpu.SemaphoreType.DMA((n, len(runs))),
+        ],
     )
     return pl.pallas_call(
-        functools.partial(sum_kernel, group, at, rows),
+        functools.partial(sum_kernel, group, runs, rows),
         grid_spec=spec,
         out_shape=jax.ShapeDtypeStruct(coarse.shape, BF16),
         input_output_aliases={2 + n: 0},
@@ -407,10 +415,12 @@
     def finish(r, codes, coarse):
         group = tuple(code for code in ROUNDS[r] if LAST[code] == r)
         arrived = [held[code] for code in group]
-        return add_arrived(group, off, arrived, codes, cols, blocks, prolong, coarse, r > 2)
+        return add_arrived(group, off, arrived, codes, cols, blocks, prolong, coarse, False)
 
     place = lax.axis_index("grp").astype(jnp.int32).reshape(1)
-    gate = codes
+    got = terms(LINKS, low, ((0, HALF),), codes, cols, blocks, prolong)
+    gate = after(codes, got[0][0])
+    lows = [send(x[0], link, groups) for x, link in zip(got, LINKS)]
     for r in range(2):
         got = terms(CALLS[r], off, ((0, total),), gate, cols, blocks, prolong)
         held.update((code, x[0]) for code, x in zip(CALLS[r], got))
@@ -422,27 +432,28 @@
     got = terms(CALLS[2], off, ((0, total),), gate, cols, blocks, prolong)
     held.update((code, x[0]) for code, x in zip(CALLS[2], got))
     gate = after(codes, got[0][0])
-    halves = ((0, HALF), (HALF, HALF))
-    direct, kept = terms(LINKS, off, halves, gate, cols, blocks, prolong, True)
+    highs, kept = terms(LINKS, high, ((0, HALF),), gate, cols, blocks, prolong, True)
 
     for r in range(2, 7):
         exchange(r)
     coarse, inv = inverses(parts, codes, place, own, table, width)
     shared = lax.all_to_all(inv, "mem", split_axis=0, concat_axis=0, tiled=True)
+    coarse = add_arrived(LINKS, low, lows, codes, cols, blocks, prolong, coarse, False)
     coarse = finish(2, codes, coarse)
+    _, (spare,) = terms(ROUNDS[6], off, ((0, 1),), codes, cols, blocks, prolong, True)
     shared = pl.pallas_call(
         copy_kernel,
         in_specs=[pl.BlockSpec(memory_space=pltpu.VMEM)],
         out_shape=jax.ShapeDtypeStruct(shared.shape, F32),
         name="keep",
     )(near(shared))
-    highs, _, coarse = lax.optimization_barrier(([x[1] for x in direct], done[5], coarse))
-    lows = [send(x[0], link, groups) for x, link in zip(direct, LINKS)]
+    highs, _, coarse = lax.optimization_barrier(([x[0] for x in highs], done[5], coarse))
     highs = [send(x, link, groups) for x, link in zip(highs, LINKS)]
     coarse = finish(5, codes, coarse)
-    coarse = finish(6, after(codes, shared), coarse)
-    coarse = sum_arrived(LINKS, 0, kept[0], lows, codes, coarse)
-    coarse = sum_arrived(LINKS, DIAG + 1, kept[1], highs, codes, coarse)
+    arrived = [held[code] for code in ROUNDS[6]]
+    runs = (0, DIAG + 1)
+    coarse = sum_arrived(ROUNDS[6], runs, spare, arrived, after(codes, shared), coarse)
+    coarse = sum_arrived(LINKS, runs[1:], kept[0], highs, codes, coarse)
     return coarse, shared.reshape(parts * rows, b // parts, b)
 
 

time: 224 us -> 248 us (1.11)
  Pallas kernels: 65.2 us -> 75.7 us
  local copies, waits for them, and re-layouts: 7.96 us -> 15.4 us
  waiting for transfers between devices: 90.8 us -> 93.5 us
  starting transfers between devices: 57.7 us -> 60.3 us
    pallas_call x4 -> x6, Pallas kernels: 29.4 us -> 40.6 us  [terms(): pl.pallas_call(functools.partial(term_kernel, group, ks, pieces, rows, ke...]
    unnamed x40 -> x56, local copies, waits for them, and re-layouts: 7.96 us -> 15.4 us
    ppermute x36, waiting for transfers between devices: 90.7 us -> 93.5 us  [send(): return lax.ppermute(x, 'grp', [(g, g ^ link) for g in range(groups)])]
    all_to_all x1, starting transfers between devices: 3.97 us -> 6.61 us  [local(): lax.all_to_all(table, 'grp', split_axis=0, concat_axis=0, tiled=True)]
  transfers between devices with their start and end apart: 38 -> 38, of which waited for: 10 -> 13; matrix products, arithmetic and copies ran while one was open for 0% -> 0% of each run, Pallas kernels for 25% -> 24%
where the time goes in v2:
time: 248 us; the launch traced here: 246 us
  waiting for transfers between devices  93.5 us (38%)
  Pallas kernels  75.7 us (31%)
  starting transfers between devices  60.3 us (24%)
  local copies, waits for them, and re-layouts  15.4 us (6%)
    ppermute x36, waiting for transfers between devices, send(): return lax.ppermute(x, 'grp', [(g, g ^ link) for g in range(groups)])  93.5 us
    ppermute x36, starting transfers between devices, send(): return lax.ppermute(x, 'grp', [(g, g ^ link) for g in range(groups)])  41.5 us
    pallas_call x6, Pallas kernels, terms(): pl.pallas_call(functools.partial(term_kernel, group, ks, pieces, rows, ke...  40.6 us
    pallas_call x3, Pallas kernels, add_arrived(): pl.pallas_call(functools.partial(add_kernel, group, ks, rows), grid_spec=...  18.2 us
    unnamed x56, local copies, waits for them, and re-layouts  15.4 us
    all_to_all x1, starting transfers between devices, local(): shared = lax.all_to_all(inv, 'mem', split_axis=0, concat_axis=0, tiled=True)  12.2 us
    pallas_call x2, Pallas kernels, sum_arrived(): pl.pallas_call(functools.partial(sum_kernel, group, runs, rows), grid_spe...  7.74 us
    all_to_all x1, starting transfers between devices, local(): lax.all_to_all(table, 'grp', split_axis=0, concat_axis=0, tiled=True)  6.61 us
  transfers between devices with their start and end apart: 38, of which 13 were waited for; matrix products, arithmetic and copies ran while one was open for 0% of the time, Pallas kernels for 24%

profile of v2, /device:TPU:1, one launch (start us, length us, event | category | flops | bytes accessed | tf_op | source)
XLA Modules:
  0.0 246.0 jit_solution(7355987136400484599)
XLA Ops:
  0.6 5.5 %shard_map.59 = (bf16[13,128,128]{2,1,0:T(8,128)(2,1)}, bf16[13,128,128]{2,1,0:T(8,128)(2,1)}, bf16[13,128,128]{2,1,0:T(8,128)(2,1)}, bf16[13,128,128]{2,1,0:T(8,128)(2,1)}) custom-call(s32[12]{0:T(128)} %codes_ref.19, s32[12,27]{1,0:T(8,128)} %cols_ref.17, bf16[12,27,128,128]{3,2,1,0:T(8,128)(2,1)} %blocks_ref.19, bf16[12,128,128]{2,1,0:T(8,128)(2,1)} %prolong_ref.19), custom_call_target="tpu_custom_call" | custom-call | flops 436207616 | bytes 3407872 | tf_op jit(solution)/shard_map/pallas_call | solution.py:127
  6.2 6.9 %shard_map.60 = (bf16[26,128,128]{2,1,0:T(8,128)(2,1)}, bf16[26,128,128]{2,1,0:T(8,128)(2,1)}, bf16[26,128,128]{2,1,0:T(8,128)(2,1)}, bf16[26,128,128]{2,1,0:T(8,128)(2,1)}) custom-call(s32[12]{0:T(128)} %codes_ref.19, s32[12,27]{1,0:T(8,128)} %cols_ref.17, bf16[12,27,128,128]{3,2,1,0:T(8,128)(2,1)} %blocks_ref.19, bf16[12,128,128]{2,1,0:T(8,128)(2,1)} %prolong_ref.19), custom_call_target="tpu_custom_call" | custom-call | flops 872415232 | bytes 6815744 | tf_op jit(solution)/shard_map/pallas_call | solution.py:127
  13.0 2.2 collective-permute-start.14
  15.2 3.8 %collective-permute-start.12 = (bf16[26,128,128]{2,1,0:T(8,128)(2,1)}, bf16[26,128,128]{2,1,0:T(8,128)(2,1)}, u32[]{:S(2)}, u32[]{:S(2)}) collective-permute-start(bf16[26,128,128]{2,1,0:T(8,128)(2,1)} %get-tuple-element.85), channel_id=1, source_target_pairs={{0,96},{8,104},{16,112},{24,120},{32,64},{40,72},{48,80},{56,88},{... | collective-permute-start | bytes 2555912 | tf_op jit(solution)/shard_map/ppermute | solution.py:392
  20.9 6.9 %shard_map.61 = (bf16[26,128,128]{2,1,0:T(8,128)(2,1)}, bf16[26,128,128]{2,1,0:T(8,128)(2,1)}, bf16[26,128,128]{2,1,0:T(8,128)(2,1)}, bf16[26,128,128]{2,1,0:T(8,128)(2,1)}) custom-call(s32[12]{0:T(128)} %codes_ref.19, s32[12,27]{1,0:T(8,128)} %cols_ref.17, bf16[12,27,128,128]{3,2,1,0:T(8,128)(2,1)} %blocks_ref.19, bf16[12,128,128]{2,1,0:T(8,128)(2,1)} %prolong_ref.19), custom_call_target="tpu_custom_call" | custom-call | flops 872415232 | bytes 6815744 | tf_op jit(solution)/shard_map/pallas_call | solution.py:127
  28.2 6.2 %collective-permute-done.14 = bf16[26,128,128]{2,1,0:T(8,128)(2,1)} collective-permute-done((bf16[26,128,128]{2,1,0:T(8,128)(2,1)}, bf16[26,128,128]{2,1,0:T(8,128)(2,1)}, u32[]{:S(2)}, u32[]{:S(2)}) %collective-permute-start.14) | collective-permute-done | bytes 852000 | tf_op jit(solution)/shard_map/ppermute | solution.py:392
  38.2 2.4 collective-permute-start
  43.3 9.4 %collective-permute-done.2 = bf16[26,128,128]{2,1,0:T(8,128)(2,1)} collective-permute-done((bf16[26,128,128]{2,1,0:T(8,128)(2,1)}, bf16[26,128,128]{2,1,0:T(8,128)(2,1)}, u32[]{:S(2)}, u32[]{:S(2)}) %collective-permute-start.2) | collective-permute-done | bytes 852000 | tf_op jit(solution)/shard_map/ppermute | solution.py:392
  54.5 2.9 %collective-permute-done.3 = bf16[26,128,128]{2,1,0:T(8,128)(2,1)} collective-permute-done((bf16[26,128,128]{2,1,0:T(8,128)(2,1)}, bf16[26,128,128]{2,1,0:T(8,128)(2,1)}, u32[]{:S(2)}, u32[]{:S(2)}) %collective-permute-start.3) | collective-permute-done | bytes 852000 | tf_op jit(solution)/shard_map/ppermute | solution.py:392
  62.0 3.5 %diag_terms.1 = (bf16[16,128,128]{2,1,0:T(8,128)(2,1)}, f32[12,128,128]{2,1,0:T(8,128)}) custom-call(s32[12]{0:T(128)} %codes_ref.19, s32[1]{0:T(128)} %bitcast.place_ref, bf16[12,27,128,128]{3,2,1,0:T(8,128)(2,1)} %blocks_ref.19, bf16[12,128,128]{2,1,0:T(8,128)(2,1)} %prolong_ref.19), custom_call_target="tpu_custom_call" | custom-call | flops 100663296 | bytes 1966080 | tf_op jit(solution)/shard_map/diag_terms/pallas_call | solution.py:162
  65.4 6.3 %shard_map.62 = (bf16[26,128,128]{2,1,0:T(8,128)(2,1)}, bf16[26,128,128]{2,1,0:T(8,128)(2,1)}, bf16[26,128,128]{2,1,0:T(8,128)(2,1)}) custom-call(s32[12]{0:T(128)} %codes_ref.19, s32[12,27]{1,0:T(8,128)} %cols_ref.17, bf16[12,27,128,128]{3,2,1,0:T(8,128)(2,1)} %blocks_ref.19, bf16[12,128,128]{2,1,0:T(8,128)(2,1)} %prolong_ref.19), custom_call_target="tpu_custom_call" | custom-call | flops 654311424 | bytes 5111808 | tf_op jit(solution)/shard_map/pallas_call | solution.py:127
  71.7 15.2 %collective-permute-done.19.refs_0_ = bf16[13,128,128]{2,1,0:T(8,128)(2,1)S(1)} collective-permute-done((bf16[13,128,128]{2,1,0:T(8,128)(2,1)}, bf16[13,128,128]{2,1,0:T(8,128)(2,1)S(1)}, u32[]{:S(2)}, u32[]{:S(2)}) %collective-permute-start.19) | collective-permute-done | bytes 426016 | tf_op jit(solution)/shard_map/ppermute | solution.py:392
  91.1 2.6 %collective-permute-start.6 = (bf16[26,128,128]{2,1,0:T(8,128)(2,1)}, bf16[26,128,128]{2,1,0:T(8,128)(2,1)}, u32[]{:S(2)}, u32[]{:S(2)}) collective-permute-start(bf16[26,128,128]{2,1,0:T(8,128)(2,1)} %copy-done.23), channel_id=1, source_target_pairs={{0,24},{8,16},{16,8},{24,0},{32,56},{40,48},{48,40},{56,32},{64,88... | collective-permute-start | bytes 2555912 | tf_op jit(solution)/shard_map/ppermute | solution.py:392
  94.7 23.3 %collective-permute-done.20.refs_1_ = bf16[13,128,128]{2,1,0:T(8,128)(2,1)S(1)} collective-permute-done((bf16[13,128,128]{2,1,0:T(8,128)(2,1)}, bf16[13,128,128]{2,1,0:T(8,128)(2,1)S(1)}, u32[]{:S(2)}, u32[]{:S(2)}) %collective-permute-start.20) | collective-permute-done | bytes 426016 | tf_op jit(solution)/shard_map/ppermute | solution.py:392
  118.7 2.7 %collective-permute-start.28 = (bf16[26,128,128]{2,1,0:T(8,128)(2,1)}, bf16[26,128,128]{2,1,0:T(8,128)(2,1)S(1)}, u32[]{:S(2)}, u32[]{:S(2)}) collective-permute-start(bf16[26,128,128]{2,1,0:T(8,128)(2,1)} %get-tuple-element.105), channel_id=1, source_target_pairs={{0,96},{8,104},{16,112},{24,120},{32,64},{40,72},{48,80},{56,88},{... | collective-permute-start | bytes 2555912 | tf_op jit(solution)/shard_map/ppermute | solution.py:392
  121.4 2.7 %collective-permute-start.30 = (bf16[26,128,128]{2,1,0:T(8,128)(2,1)}, bf16[26,128,128]{2,1,0:T(8,128)(2,1)}, u32[]{:S(2)}, u32[]{:S(2)}) collective-permute-start(bf16[26,128,128]{2,1,0:T(8,128)(2,1)} %collective-permute-done.27), channel_id=1, source_target_pairs={{0,24},{8,16},{16,8},{24,0},{32,56},{40,48},{48,40},{56,32},{64,88... | collective-permute-start | bytes 2555912 | tf_op jit(solution)/shard_map/ppermute | solution.py:392
  125.5 5.9 %collective-permute-done.21.refs_2_ = bf16[13,128,128]{2,1,0:T(8,128)(2,1)S(1)} collective-permute-done((bf16[13,128,128]{2,1,0:T(8,128)(2,1)S(1)}, bf16[13,128,128]{2,1,0:T(8,128)(2,1)S(1)}, u32[]{:S(2)}, u32[]{:S(2)}) %collective-permute-start.21) | collective-permute-done | bytes 426016 | tf_op jit(solution)/shard_map/ppermute | solution.py:392
  132.2 3.8 %collective-permute-done.28 = bf16[26,128,128]{2,1,0:T(8,128)(2,1)S(1)} collective-permute-done((bf16[26,128,128]{2,1,0:T(8,128)(2,1)}, bf16[26,128,128]{2,1,0:T(8,128)(2,1)S(1)}, u32[]{:S(2)}, u32[]{:S(2)}) %collective-permute-start.28) | collective-permute-done | bytes 852000 | tf_op jit(solution)/shard_map/ppermute | solution.py:392
  136.0 3.4 %collective-permute-start.11 = (bf16[26,128,128]{2,1,0:T(8,128)(2,1)}, bf16[26,128,128]{2,1,0:T(8,128)(2,1)S(1)}, u32[]{:S(2)}, u32[]{:S(2)}) collective-permute-start(bf16[26,128,128]{2,1,0:T(8,128)(2,1)} %collective-permute-done.7), channel_id=1, source_target_pairs={{0,96},{8,104},{16,112},{24,120},{32,64},{40,72},{48,80},{56,88},{... | collective-permute-start | bytes 2555912 | tf_op jit(solution)/shard_map/ppermute | solution.py:392
  141.2 6.6 %all-to-all-start = ((bf16[16,128,128]{2,1,0:T(8,128)(2,1)}), bf16[16,128,128]{2,1,0:T(8,128)(2,1)}, u32[]{:S(2)}, u32[]{:S(2)}) async-start(bf16[16,128,128]{2,1,0:T(8,128)(2,1)} %get-tuple-element.94), calls=%async_computation | async-start | bytes 1048576 | tf_op jit(solution)/shard_map/all_to_all | solution.py:430
  150.5 16.2 %collective-permute-done.22.refs_3_ = bf16[13,128,128]{2,1,0:T(8,128)(2,1)} collective-permute-done((bf16[13,128,128]{2,1,0:T(8,128)(2,1)}, bf16[13,128,128]{2,1,0:T(8,128)(2,1)}, u32[]{:S(2)}, u32[]{:S(2)}) %collective-permute-start.22) | collective-permute-done | bytes 426016 | tf_op jit(solution)/shard_map/ppermute | solution.py:392
  166.7 4.9 %collective-permute-done.10.refs_2_ = bf16[26,128,128]{2,1,0:T(8,128)(2,1)S(1)} collective-permute-done((bf16[26,128,128]{2,1,0:T(8,128)(2,1)}, bf16[26,128,128]{2,1,0:T(8,128)(2,1)S(1)}, u32[]{:S(2)}, u32[]{:S(2)}) %collective-permute-start.10) | collective-permute-done | bytes 852000 | tf_op jit(solution)/shard_map/ppermute | solution.py:392
  173.0 4.7 %inverses.1 = (bf16[12,27,128,128]{3,2,1,0:T(8,128)(2,1)}, f32[8,12,16,128]{3,2,1,0:T(8,128)}) custom-call(s32[12]{0:T(128)} %codes_ref.19, s32[1]{0:T(128)} %bitcast.place_ref, f32[12,128,128]{2,1,0:T(8,128)} %get-tuple-element.64.own_ref, bf16[16,128,128]{2,1,0:T(8,128)(2,1)} %all-to-all-done.arrived_ref), custom_call_target="tpu_custom_call" | custom-call | flops 603979776 | bytes 2359296 | tf_op jit(solution)/shard_map/inverses/pallas_call | solution.py:212
  177.8 12.2 %all-to-all-start.1 = ((f32[8,12,16,128]{3,2,1,0:T(8,128)}), f32[8,12,16,128]{3,2,1,0:T(8,128)S(1)}, u32[]{:S(2)}, u32[]{:S(2)}) async-start(f32[8,12,16,128]{3,2,1,0:T(8,128)} %get-tuple-element.100), calls=%async_computation.1 | async-start | bytes 1572864 | tf_op jit(solution)/shard_map/all_to_all | solution.py:440
  190.0 6.9 %shard_map.63 = (bf16[13,128,128]{2,1,0:T(8,128)(2,1)}, bf16[13,128,128]{2,1,0:T(8,128)(2,1)}, bf16[13,128,128]{2,1,0:T(8,128)(2,1)}, bf16[13,128,128]{2,1,0:T(8,128)(2,1)}, f32[4,13,128,128]{3,2,1,0:T(8,128)}) custom-call(s32[12]{0:T(128)} %codes_ref.19, s32[12,27]{1,0:T(8,128)} %cols_ref.17, bf16[12,27,128,128]{3,2,1,0:T(8,128)(2,1)} %blocks_ref.19, ...), custom_call_target="tpu_custom_call" | custom-call | flops 436207616 | bytes 3407872 | tf_op jit(solution)/shard_map/pallas_call | solution.py:127
  199.9 5.4 %shard_map.64.refs_3_ = bf16[12,27,128,128]{3,2,1,0:T(8,128)(2,1)} custom-call(s32[12]{0:T(128)} %codes_ref.19, s32[12,27]{1,0:T(8,128)} %cols_ref.17, bf16[12,128,128]{2,1,0:T(8,128)(2,1)} %prolong_ref.19, bf16[12,27,128,128]{3,2,1,0:T(8,128)(2,1)} %blocks_ref.19, bf16[13,128,128]{2,1,0:T(8,128)(2,1)S(1)} %copy-done.16, ...), custom_call_target="tpu_custom_call", output_to_operand_aliasing={{}: (8, {})} | custom-call | flops 436207616 | bytes 5111808 | tf_op jit(solution)/shard_map/pallas_call | solution.py:300
  205.4 6.2 %shard_map.65.refs_4_ = bf16[12,27,128,128]{3,2,1,0:T(8,128)(2,1)} custom-call(s32[12]{0:T(128)} %codes_ref.19, s32[12,27]{1,0:T(8,128)} %cols_ref.17, bf16[12,128,128]{2,1,0:T(8,128)(2,1)} %prolong_ref.19, bf16[12,27,128,128]{3,2,1,0:T(8,128)(2,1)} %blocks_ref.19, bf16[26,128,128]{2,1,0:T(8,128)(2,1)S(1)} %copy-done.10, ...), custom_call_target="tpu_custom_call", output_to_operand_aliasing={{}: (7, {})} | custom-call | flops 654311424 | bytes 7962624 | tf_op jit(solution)/shard_map/pallas_call | solution.py:300
  215.2 2.3 collective-permute-start.26
  217.5 8.2 %shard_map.66 = (bf16[1,128,128]{2,1,0:T(8,128)(2,1)}, bf16[1,128,128]{2,1,0:T(8,128)(2,1)}, bf16[1,128,128]{2,1,0:T(8,128)(2,1)}, bf16[1,128,128]{2,1,0:T(8,128)(2,1)}, f32[4,26,128,128]{3,2,1,0:T(8,128)}) custom-call(s32[12]{0:T(128)} %codes_ref.19, s32[12,27]{1,0:T(8,128)} %cols_ref.17, bf16[12,27,128,128]{3,2,1,0:T(8,128)(2,1)} %blocks_ref.19, ...), custom_call_target="tpu_custom_call" | custom-call | flops 872415232 | bytes 6815744 | tf_op jit(solution)/shard_map/pallas_call | solution.py:127
  231.4 6.6 %shard_map.67.refs_4_ = bf16[12,27,128,128]{3,2,1,0:T(8,128)(2,1)} custom-call(s32[12]{0:T(128)} %codes_ref.19, s32[12,27]{1,0:T(8,128)} %cols_ref.17, bf16[12,128,128]{2,1,0:T(8,128)(2,1)} %prolong_ref.19, bf16[12,27,128,128]{3,2,1,0:T(8,128)(2,1)} %blocks_ref.19, bf16[26,128,128]{2,1,0:T(8,128)(2,1)S(1)} %copy-done.6, ...), custom_call_target="tpu_custom_call", output_to_operand_aliasing={{}: (8, {})} | custom-call | flops 872415232 | bytes 10616832 | tf_op jit(solution)/shard_map/pallas_call | solution.py:300
  238.1 4.5 %shard_map.68.refs_4_ = bf16[12,27,128,128]{3,2,1,0:T(8,128)(2,1)} custom-call(s32[12]{0:T(128)} %codes_ref.19, f32[4,26,128,128]{3,2,1,0:T(8,128)S(1)} %bitcast.3, bf16[26,128,128]{2,1,0:T(8,128)(2,1)} %collective-permute-done.32.refs_0_, bf16[26,128,128]{2,1,0:T(8,128)(2,1)} %collective-permute-done.33.refs_1_, ...), custom_call_target="tpu_custom_call", output_to_operand_aliasing={{}: (6, {})} | custom-call | flops 1703936 | bytes 13631488 | tf_op jit(solution)/shard_map/pallas_call | solution.py:363
  242.7 3.2 %shard_map.69 = bf16[12,27,128,128]{3,2,1,0:T(8,128)(2,1)} custom-call(s32[12]{0:T(128)} %codes_ref.19, f32[4,13,128,128]{3,2,1,0:T(8,128)S(1)} %copy-done, bf16[13,128,128]{2,1,0:T(8,128)(2,1)} %collective-permute-done.23.refs_0_, bf16[13,128,128]{2,1,0:T(8,128)(2,1)} %collective-permute-done.24.refs_1_, ...), custom_call_target="tpu_custom_call", output_to_operand_aliasing={{}: (6, {})} | custom-call | flops 851968 | bytes 6815744 | tf_op jit(solution)/shard_map/pallas_call | solution.py:363
  (115 shorter events, 41.6 us)
Async XLA Ops:
  13.0 21.4 %collective-permute-start.14 = (bf16[26,128,128]{2,1,0:T(8,128)(2,1)}, bf16[26,128,128]{2,1,0:T(8,128)(2,1)}, u32[]{:S(2)}, u32[]{:S(2)}) collective-permute-start(bf16[26,128,128]{2,1,0:T(8,128)(2,1)} %get-tuple-element.60), channel_id=1, source_target_pairs={{0,8},{8,0},{16,24},{24,16},{32,40},{40,32},{48,56},{56,48},{64,72... | collective-permute-start | bytes 2555912 | tf_op jit(solution)/shard_map/ppermute | solution.py:392
  15.2 23.0 %collective-permute-start.12 = (bf16[26,128,128]{2,1,0:T(8,128)(2,1)}, bf16[26,128,128]{2,1,0:T(8,128)(2,1)}, u32[]{:S(2)}, u32[]{:S(2)}) collective-permute-start(bf16[26,128,128]{2,1,0:T(8,128)(2,1)} %get-tuple-element.85), channel_id=1, source_target_pairs={{0,96},{8,104},{16,112},{24,120},{32,64},{40,72},{48,80},{56,88},{... | collective-permute-start | bytes 2555912 | tf_op jit(solution)/shard_map/ppermute | solution.py:392
  19.0 21.6 %collective-permute-start.13 = (bf16[26,128,128]{2,1,0:T(8,128)(2,1)}, bf16[26,128,128]{2,1,0:T(8,128)(2,1)}, u32[]{:S(2)}, u32[]{:S(2)}) collective-permute-start(bf16[26,128,128]{2,1,0:T(8,128)(2,1)} %get-tuple-element.86), channel_id=1, source_target_pairs={{0,32},{8,40},{16,48},{24,56},{32,0},{40,8},{48,16},{56,24},{64,96... | collective-permute-start | bytes 2555912 | tf_op jit(solution)/shard_map/ppermute | solution.py:392
  19.0 23.5 %collective-permute-start.15 = (bf16[26,128,128]{2,1,0:T(8,128)(2,1)}, bf16[26,128,128]{2,1,0:T(8,128)(2,1)}, u32[]{:S(2)}, u32[]{:S(2)}) collective-permute-start(bf16[26,128,128]{2,1,0:T(8,128)(2,1)} %get-tuple-element.87), channel_id=1, source_target_pairs={{0,24},{8,16},{16,8},{24,0},{32,56},{40,48},{48,40},{56,32},{64,88... | collective-permute-start | bytes 2555912 | tf_op jit(solution)/shard_map/ppermute | solution.py:392
  27.8 24.9 %collective-permute-start.2 = (bf16[26,128,128]{2,1,0:T(8,128)(2,1)}, bf16[26,128,128]{2,1,0:T(8,128)(2,1)}, u32[]{:S(2)}, u32[]{:S(2)}) collective-permute-start(bf16[26,128,128]{2,1,0:T(8,128)(2,1)} %get-tuple-element.62), channel_id=1, source_target_pairs={{0,8},{8,0},{16,24},{24,16},{32,40},{40,32},{48,56},{56,48},{64,72... | collective-permute-start | bytes 2555912 | tf_op jit(solution)/shard_map/ppermute | solution.py:392
  34.4 23.0 %collective-permute-start.3 = (bf16[26,128,128]{2,1,0:T(8,128)(2,1)}, bf16[26,128,128]{2,1,0:T(8,128)(2,1)}, u32[]{:S(2)}, u32[]{:S(2)}) collective-permute-start(bf16[26,128,128]{2,1,0:T(8,128)(2,1)} %get-tuple-element.76), channel_id=1, source_target_pairs={{0,32},{8,40},{16,48},{24,56},{32,0},{40,8},{48,16},{56,24},{64,96... | collective-permute-start | bytes 2555912 | tf_op jit(solution)/shard_map/ppermute | solution.py:392
  42.5 46.1 %collective-permute-start.16 = (bf16[26,128,128]{2,1,0:T(8,128)(2,1)}, bf16[26,128,128]{2,1,0:T(8,128)(2,1)S(1)}, u32[]{:S(2)}, u32[]{:S(2)}) collective-permute-start(bf16[26,128,128]{2,1,0:T(8,128)(2,1)} %collective-permute-done.13), channel_id=1, source_target_pairs={{0,24},{8,16},{16,8},{24,0},{32,56},{40,48},{48,40},{56,32},{64,88... | collective-permute-start | bytes 2555912 | tf_op jit(solution)/shard_map/ppermute | solution.py:392
  52.7 37.5 %collective-permute-start.17 = (bf16[26,128,128]{2,1,0:T(8,128)(2,1)}, bf16[26,128,128]{2,1,0:T(8,128)(2,1)S(1)}, u32[]{:S(2)}, u32[]{:S(2)}) collective-permute-start(bf16[26,128,128]{2,1,0:T(8,128)(2,1)} %collective-permute-done.14), channel_id=1, source_target_pairs={{0,32},{8,40},{16,48},{24,56},{32,0},{40,8},{48,16},{56,24},{64,96... | collective-permute-start | bytes 2555912 | tf_op jit(solution)/shard_map/ppermute | solution.py:392
  57.4 36.2 %collective-permute-start.18 = (bf16[26,128,128]{2,1,0:T(8,128)(2,1)}, bf16[26,128,128]{2,1,0:T(8,128)(2,1)S(1)}, u32[]{:S(2)}, u32[]{:S(2)}) collective-permute-start(bf16[26,128,128]{2,1,0:T(8,128)(2,1)} %collective-permute-done.15), channel_id=1, source_target_pairs={{0,96},{8,104},{16,112},{24,120},{32,64},{40,72},{48,80},{56,88},{... | collective-permute-start | bytes 2555912 | tf_op jit(solution)/shard_map/ppermute | solution.py:392
  59.2 35.5 %collective-permute-start.27 = (bf16[26,128,128]{2,1,0:T(8,128)(2,1)}, bf16[26,128,128]{2,1,0:T(8,128)(2,1)}, u32[]{:S(2)}, u32[]{:S(2)}) collective-permute-start(bf16[26,128,128]{2,1,0:T(8,128)(2,1)} %collective-permute-done.12), channel_id=1, source_target_pairs={{0,8},{8,0},{16,24},{24,16},{32,40},{40,32},{48,56},{56,48},{64,72... | collective-permute-start | bytes 2555912 | tf_op jit(solution)/shard_map/ppermute | solution.py:392
  61.9 25.0 %collective-permute-start.19 = (bf16[13,128,128]{2,1,0:T(8,128)(2,1)}, bf16[13,128,128]{2,1,0:T(8,128)(2,1)S(1)}, u32[]{:S(2)}, u32[]{:S(2)}) collective-permute-start(bf16[13,128,128]{2,1,0:T(8,128)(2,1)} %get-tuple-element.58), channel_id=1, source_target_pairs={{0,8},{8,0},{16,24},{24,16},{32,40},{40,32},{48,56},{56,48},{64,72... | collective-permute-start | bytes 1277960 | tf_op jit(solution)/shard_map/ppermute | solution.py:392
  87.7 33.7 %collective-permute-start.4 = (bf16[26,128,128]{2,1,0:T(8,128)(2,1)}, bf16[26,128,128]{2,1,0:T(8,128)(2,1)}, u32[]{:S(2)}, u32[]{:S(2)}) collective-permute-start(bf16[26,128,128]{2,1,0:T(8,128)(2,1)} %copy-done.24), channel_id=1, source_target_pairs={{0,96},{8,104},{16,112},{24,120},{32,64},{40,72},{48,80},{56,88},{... | collective-permute-start | bytes 2555912 | tf_op jit(solution)/shard_map/ppermute | solution.py:392
  89.5 31.8 %collective-permute-start.5 = (bf16[26,128,128]{2,1,0:T(8,128)(2,1)}, bf16[26,128,128]{2,1,0:T(8,128)(2,1)}, u32[]{:S(2)}, u32[]{:S(2)}) collective-permute-start(bf16[26,128,128]{2,1,0:T(8,128)(2,1)} %get-tuple-element.78), channel_id=1, source_target_pairs={{0,8},{8,0},{16,24},{24,16},{32,40},{40,32},{48,56},{56,48},{64,72... | collective-permute-start | bytes 2555912 | tf_op jit(solution)/shard_map/ppermute | solution.py:392
  91.1 33.0 %collective-permute-start.6 = (bf16[26,128,128]{2,1,0:T(8,128)(2,1)}, bf16[26,128,128]{2,1,0:T(8,128)(2,1)}, u32[]{:S(2)}, u32[]{:S(2)}) collective-permute-start(bf16[26,128,128]{2,1,0:T(8,128)(2,1)} %copy-done.23), channel_id=1, source_target_pairs={{0,24},{8,16},{16,8},{24,0},{32,56},{40,48},{48,40},{56,32},{64,88... | collective-permute-start | bytes 2555912 | tf_op jit(solution)/shard_map/ppermute | solution.py:392
  94.6 23.4 %collective-permute-start.20 = (bf16[13,128,128]{2,1,0:T(8,128)(2,1)}, bf16[13,128,128]{2,1,0:T(8,128)(2,1)S(1)}, u32[]{:S(2)}, u32[]{:S(2)}) collective-permute-start(bf16[13,128,128]{2,1,0:T(8,128)(2,1)} %get-tuple-element.91), channel_id=1, source_target_pairs={{0,24},{8,16},{16,8},{24,0},{32,56},{40,48},{48,40},{56,32},{64,88... | collective-permute-start | bytes 1277960 | tf_op jit(solution)/shard_map/ppermute | solution.py:392
  94.7 29.4 %collective-permute-start.7 = (bf16[26,128,128]{2,1,0:T(8,128)(2,1)}, bf16[26,128,128]{2,1,0:T(8,128)(2,1)}, u32[]{:S(2)}, u32[]{:S(2)}) collective-permute-start(bf16[26,128,128]{2,1,0:T(8,128)(2,1)} %get-tuple-element.80), channel_id=1, source_target_pairs={{0,32},{8,40},{16,48},{24,56},{32,0},{40,8},{48,16},{56,24},{64,96... | collective-permute-start | bytes 2555912 | tf_op jit(solution)/shard_map/ppermute | solution.py:392
  124.1 25.1 %collective-permute-start.31 = (bf16[26,128,128]{2,1,0:T(8,128)(2,1)}, bf16[26,128,128]{2,1,0:T(8,128)(2,1)}, u32[]{:S(2)}, u32[]{:S(2)}) collective-permute-start(bf16[26,128,128]{2,1,0:T(8,128)(2,1)} %collective-permute-done.2), channel_id=1, source_target_pairs={{0,32},{8,40},{16,48},{24,56},{32,0},{40,8},{48,16},{56,24},{64,96... | collective-permute-start | bytes 2555912 | tf_op jit(solution)/shard_map/ppermute | solution.py:392
  132.2 39.4 %collective-permute-start.10 = (bf16[26,128,128]{2,1,0:T(8,128)(2,1)}, bf16[26,128,128]{2,1,0:T(8,128)(2,1)S(1)}, u32[]{:S(2)}, u32[]{:S(2)}) collective-permute-start(bf16[26,128,128]{2,1,0:T(8,128)(2,1)} %collective-permute-done.6), channel_id=1, source_target_pairs={{0,32},{8,40},{16,48},{24,56},{32,0},{40,8},{48,16},{56,24},{64,96... | collective-permute-start | bytes 2555912 | tf_op jit(solution)/shard_map/ppermute | solution.py:392
  136.0 35.9 %collective-permute-start.11 = (bf16[26,128,128]{2,1,0:T(8,128)(2,1)}, bf16[26,128,128]{2,1,0:T(8,128)(2,1)S(1)}, u32[]{:S(2)}, u32[]{:S(2)}) collective-permute-start(bf16[26,128,128]{2,1,0:T(8,128)(2,1)} %collective-permute-done.7), channel_id=1, source_target_pairs={{0,96},{8,104},{16,112},{24,120},{32,64},{40,72},{48,80},{56,88},{... | collective-permute-start | bytes 2555912 | tf_op jit(solution)/shard_map/ppermute | solution.py:392
  140.3 31.8 %collective-permute-start.8 = (bf16[26,128,128]{2,1,0:T(8,128)(2,1)}, bf16[26,128,128]{2,1,0:T(8,128)(2,1)S(1)}, u32[]{:S(2)}, u32[]{:S(2)}) collective-permute-start(bf16[26,128,128]{2,1,0:T(8,128)(2,1)} %collective-permute-done.4), channel_id=1, source_target_pairs={{0,8},{8,0},{16,24},{24,16},{32,40},{40,32},{48,56},{56,48},{64,72... | collective-permute-start | bytes 2555912 | tf_op jit(solution)/shard_map/ppermute | solution.py:392
  140.3 26.4 %collective-permute-start.22 = (bf16[13,128,128]{2,1,0:T(8,128)(2,1)}, bf16[13,128,128]{2,1,0:T(8,128)(2,1)}, u32[]{:S(2)}, u32[]{:S(2)}) collective-permute-start(bf16[13,128,128]{2,1,0:T(8,128)(2,1)} %get-tuple-element.93), channel_id=1, source_target_pairs={{0,96},{8,104},{16,112},{24,120},{32,64},{40,72},{48,80},{56,88},{... | collective-permute-start | bytes 1277960 | tf_op jit(solution)/shard_map/ppermute | solution.py:392
  141.2 31.8 %all-to-all-start = ((bf16[16,128,128]{2,1,0:T(8,128)(2,1)}), bf16[16,128,128]{2,1,0:T(8,128)(2,1)}, u32[]{:S(2)}, u32[]{:S(2)}) async-start(bf16[16,128,128]{2,1,0:T(8,128)(2,1)} %get-tuple-element.94), calls=%async_computation | async-start | bytes 1048576 | tf_op jit(solution)/shard_map/all_to_all | solution.py:430
  149.2 62.4 %collective-permute-start.9 = (bf16[26,128,128]{2,1,0:T(8,128)(2,1)}, bf16[26,128,128]{2,1,0:T(8,128)(2,1)S(1)}, u32[]{:S(2)}, u32[]{:S(2)}) collective-permute-start(bf16[26,128,128]{2,1,0:T(8,128)(2,1)} %collective-permute-done.5), channel_id=1, source_target_pairs={{0,24},{8,16},{16,8},{24,0},{32,56},{40,48},{48,40},{56,32},{64,88... | collective-permute-start | bytes 2555912 | tf_op jit(solution)/shard_map/ppermute | solution.py:392
  166.7 45.8 %collective-permute-start.32 = (bf16[26,128,128]{2,1,0:T(8,128)(2,1)}, bf16[26,128,128]{2,1,0:T(8,128)(2,1)}, u32[]{:S(2)}, u32[]{:S(2)}) collective-permute-start(bf16[26,128,128]{2,1,0:T(8,128)(2,1)} %copy-done.21), channel_id=1, source_target_pairs={{0,8},{8,0},{16,24},{24,16},{32,40},{40,32},{48,56},{56,48},{64,72... | collective-permute-start | bytes 2555912 | tf_op jit(solution)/shard_map/ppermute | solution.py:392
  171.6 41.9 %collective-permute-start.33 = (bf16[26,128,128]{2,1,0:T(8,128)(2,1)}, bf16[26,128,128]{2,1,0:T(8,128)(2,1)}, u32[]{:S(2)}, u32[]{:S(2)}) collective-permute-start(bf16[26,128,128]{2,1,0:T(8,128)(2,1)} %copy-done.22), channel_id=1, source_target_pairs={{0,24},{8,16},{16,8},{24,0},{32,56},{40,48},{48,40},{56,32},{64,88... | collective-permute-start | bytes 2555912 | tf_op jit(solution)/shard_map/ppermute | solution.py:392
  171.8 43.3 %collective-permute-start.34 = (bf16[26,128,128]{2,1,0:T(8,128)(2,1)}, bf16[26,128,128]{2,1,0:T(8,128)(2,1)}, u32[]{:S(2)}, u32[]{:S(2)}) collective-permute-start(bf16[26,128,128]{2,1,0:T(8,128)(2,1)} %collective-permute-done.30), channel_id=1, source_target_pairs={{0,32},{8,40},{16,48},{24,56},{32,0},{40,8},{48,16},{56,24},{64,96... | collective-permute-start | bytes 2555912 | tf_op jit(solution)/shard_map/ppermute | solution.py:392
  172.1 65.9 %collective-permute-start.35 = (bf16[26,128,128]{2,1,0:T(8,128)(2,1)}, bf16[26,128,128]{2,1,0:T(8,128)(2,1)}, u32[]{:S(2)}, u32[]{:S(2)}) collective-permute-start(bf16[26,128,128]{2,1,0:T(8,128)(2,1)} %collective-permute-done.31), channel_id=1, source_target_pairs={{0,96},{8,104},{16,112},{24,120},{32,64},{40,72},{48,80},{56,88},{... | collective-permute-start | bytes 2555912 | tf_op jit(solution)/shard_map/ppermute | solution.py:392
  177.8 47.9 %all-to-all-start.1 = ((f32[8,12,16,128]{3,2,1,0:T(8,128)}), f32[8,12,16,128]{3,2,1,0:T(8,128)S(1)}, u32[]{:S(2)}, u32[]{:S(2)}) async-start(f32[8,12,16,128]{3,2,1,0:T(8,128)} %get-tuple-element.100), calls=%async_computation.1 | async-start | bytes 1572864 | tf_op jit(solution)/shard_map/all_to_all | solution.py:440
  211.6 31.1 %collective-permute-start.23 = (bf16[13,128,128]{2,1,0:T(8,128)(2,1)}, bf16[13,128,128]{2,1,0:T(8,128)(2,1)}, u32[]{:S(2)}, u32[]{:S(2)}) collective-permute-start(bf16[13,128,128]{2,1,0:T(8,128)(2,1)} %get-tuple-element.96), channel_id=1, source_target_pairs={{0,8},{8,0},{16,24},{24,16},{32,40},{40,32},{48,56},{56,48},{64,72... | collective-permute-start | bytes 1277960 | tf_op jit(solution)/shard_map/ppermute | solution.py:392
  212.5 30.1 %collective-permute-start.24 = (bf16[13,128,128]{2,1,0:T(8,128)(2,1)}, bf16[13,128,128]{2,1,0:T(8,128)(2,1)}, u32[]{:S(2)}, u32[]{:S(2)}) collective-permute-start(bf16[13,128,128]{2,1,0:T(8,128)(2,1)} %get-tuple-element.97), channel_id=1, source_target_pairs={{0,24},{8,16},{16,8},{24,0},{32,56},{40,48},{48,40},{56,32},{64,88... | collective-permute-start | bytes 1277960 | tf_op jit(solution)/shard_map/ppermute | solution.py:392
  213.5 29.1 %collective-permute-start.25 = (bf16[13,128,128]{2,1,0:T(8,128)(2,1)}, bf16[13,128,128]{2,1,0:T(8,128)(2,1)}, u32[]{:S(2)}, u32[]{:S(2)}) collective-permute-start(bf16[13,128,128]{2,1,0:T(8,128)(2,1)} %get-tuple-element.98), channel_id=1, source_target_pairs={{0,32},{8,40},{16,48},{24,56},{32,0},{40,8},{48,16},{56,24},{64,96... | collective-permute-start | bytes 1277960 | tf_op jit(solution)/shard_map/ppermute | solution.py:392
  215.2 27.5 %collective-permute-start.26 = (bf16[13,128,128]{2,1,0:T(8,128)(2,1)}, bf16[13,128,128]{2,1,0:T(8,128)(2,1)}, u32[]{:S(2)}, u32[]{:S(2)}) collective-permute-start(bf16[13,128,128]{2,1,0:T(8,128)(2,1)} %get-tuple-element.99), channel_id=1, source_target_pairs={{0,96},{8,104},{16,112},{24,120},{32,64},{40,72},{48,80},{56,88},{... | collective-permute-start | bytes 1277960 | tf_op jit(solution)/shard_map/ppermute | solution.py:392
  (34 other events, 311.0 us)
